TPU v7x, 128 devices: a whole 4x4x4 slice. The times are simulated.
128 devices in a mesh: fsdp: 8 (over x, core), context: 4 (over z), tensor: 4 (over y).
Axes of the slice: x: 4, y: 4, z: 4, core: 2. Of those that a mesh axis runs over, the one named last changes fastest.
Arguments:
- tokens: bfloat16 [32, 1024, 1536], P('fsdp', 'context'), may hold values from -6 to 6
- output_cotangent: bfloat16 [32, 1024, 1536], P('fsdp', 'context'), may hold values from -6 to 6
- segments: int32 [32, 1024], P('fsdp', 'context'), may hold values from 0 to 3, never falling along the last dimension, each value on 1 to 512 neighbouring positions
- sequence_adapter: int32 [32], P('fsdp'), may hold values from 0 to 7
- input_norm_gain: float32 [1536], replicated, may hold values from 0.1 to 1.9
- gate_x_projection_weight: bfloat16 [1536, 2, 3072], P(('fsdp', 'context'), None, 'tensor'), may hold values from -0.15625 to 0.15625
- bc_projection_weight: bfloat16 [1536, 256], P(('fsdp', 'context')), may hold values from -0.15625 to 0.15625
- step_projection_weight: bfloat16 [1536, 48], P(('fsdp', 'context'), 'tensor'), may hold values from -0.15625 to 0.15625
- x_convolution_taps: float32 [4, 3072], P(None, 'tensor'), may hold values from -3 to 3
- x_convolution_bias: float32 [3072], P('tensor'), may hold values from -3 to 3
- bc_convolution_taps: float32 [4, 256], replicated, may hold values from -3 to 3
- bc_convolution_bias: float32 [256], replicated, may hold values from -3 to 3
- step_size_bias: float32 [48], P('tensor'), may hold values from -4.6 to -2.2
- log_decay_rate: float32 [48], P('tensor'), may hold values from -3 to 0.7
- head_skip_gain: float32 [48], P('tensor'), may hold values from 0.5 to 1.5
- gated_norm_gain: float32 [3072], P('tensor'), may hold values from 0.1 to 1.9
- output_projection_weight: bfloat16 [3072, 1536], P('tensor', ('fsdp', 'context')), may hold values from -0.109375 to 0.109375
- in_adapter_down: bfloat16 [8, 1536, 16], replicated, may hold values from -0.15625 to 0.15625
- in_adapter_up: bfloat16 [8, 16, 2, 3072], P(None, None, None, 'tensor'), may hold values from -0.75 to 0.75
- out_adapter_down: bfloat16 [8, 3072, 16], P(None, 'tensor'), may hold values from -0.109375 to 0.109375
- out_adapter_up: bfloat16 [8, 16, 1536], replicated, may hold values from -0.75 to 0.75
Outputs:
- layer_out: bfloat16 [32, 1024, 1536], P('fsdp', 'context')
- grad_tokens: float32 [32, 1024, 1536], P('fsdp', 'context')
- grad_lora_in_a: float32 [8, 1536, 16], replicated
- grad_lora_in_b: float32 [8, 16, 2, 3072], P(None, None, None, 'tensor')
- grad_lora_out_a: float32 [8, 3072, 16], P(None, 'tensor')
- grad_lora_out_b: float32 [8, 16, 1536], replicated
Inputs may be any that keep to these rules, and one draw needn't show every extreme that they name: `segments`: segment numbers never fall along a sequence, every one of 0 .. 3 occurs in each sequence, and one document has exactly 512 tokens.
All inputs are finite; a program needn't handle non-finite values.
Results may differ from a plain program's by a relative error of at most 0.0089.
Values may be sent and summed in bfloat16 or wider, within the bound.
No kernel may reach another device: no remote copies, remote signals or barrier semaphores. Data moves between devices by JAX's collectives and lax.ppermute only.
A program may use at most 192 MiB of HBM per device.

v0:
```python
import jax
import jax.numpy as jnp
from jax import lax
from jax.sharding import PartitionSpec as P

INNER_CHANNELS = 3072


EPS_NORM = 1e-05


def gather_turned(arrays, axis, dims):
    turned = [jnp.moveaxis(a, dim, 0) for a, dim in zip(arrays, dims)]
    widths = [t[0].size for t in turned]
    both = jnp.concatenate([t.reshape(-1, w) for t, w in zip(turned, widths)], axis=1)
    filled = lax.all_gather(both, axis, axis=0, tiled=True)
    pieces = jnp.split(filled, [sum(widths[:k]) for k in range(1, len(widths))], axis=1)
    return tuple(
        (
            jnp.moveaxis(b.reshape(-1, *t.shape[1:]), 0, dim)
            for b, t, dim in zip(pieces, turned, dims)
        )
    )


def from_behind(block, axis, distance):
    devices = range(lax.axis_size(axis))
    route = [(i - distance, i) for i in devices if i - distance in devices]
    return lax.ppermute(block, axis, route)


def carried_in(value, axis, combine, identity):
    size, position = (lax.axis_size(axis), lax.axis_index(axis))
    everything = jax.tree.map(lambda part: lax.all_gather(part, axis), value)
    start = jax.tree.map(
        lambda part, zero: jnp.broadcast_to(jnp.asarray(zero, part.dtype), part.shape),
        value,
        identity,
    )

    def lap(k, before):
        reached = k < position
        new = combine(before, jax.tree.map(lambda part: part[k], everything))
        return jax.tree.map(lambda a, b: jnp.where(reached, a, b), new, before)

    return lax.fori_loop(0, size, lap, start)


def sent_to_all(value, axis):
    size = lax.axis_size(axis)
    return lax.all_to_all(
        jnp.broadcast_to(value[None], (size, *value.shape)), axis, 0, 0, tiled=True
    )


def of_everyone(value, axis):
    everything = sent_to_all(value, axis)
    return jnp.sum(everything, axis=0)


def split_up(value, dim, size):
    before, after = (value.shape[:dim], value.shape[dim + 1 :])
    return jnp.moveaxis(value.reshape(*before, size, -1, *after), dim, 0)


def summed_on_arrival(value, axis, dim):
    size = lax.axis_size(axis)
    pieces = lax.all_to_all(split_up(value, dim, size), axis, 0, 0, tiled=True)
    return jnp.sum(pieces, axis=0)


def entering(value, axis, join, neutral):
    count = lax.axis_size(axis)
    place = lax.axis_index(axis)
    ahead = count - 1 - place
    gathered = jax.tree.map(
        lambda a, kind: lax.all_gather(a.astype(kind), axis),
        value,
        jax.tree.map(lambda a: jnp.bfloat16 if a.dtype == jnp.float32 else a.dtype, value),
    )
    state = jax.tree.map(lambda a, e: jnp.zeros_like(a) + jnp.asarray(e, a.dtype), value, neutral)

    def one(lap, state):
        source = count - 1 - lap
        return join(
            state,
            jax.tree.map(
                lambda a, own: lax.dynamic_index_in_dim(a, source, 0, False).astype(own.dtype),
                gathered,
                value,
            ),
        )

    return lax.fori_loop(0, ahead, one, state)


def conv_silu(padded, padded_seg, seg_ids, tap_weight, tap_bias):
    length = seg_ids.shape[-1]
    running_sum = tap_bias
    for offset in range(tap_weight.shape[0]):
        agrees = (padded_seg[..., offset : offset + length] == seg_ids).astype(jnp.float32)
        running_sum = (
            running_sum
            + tap_weight[offset] * padded[..., offset : offset + length, :] * agrees[..., None]
        )
    return jax.nn.silu(running_sum)


def ssd_parts(
    x_heads,
    b_values,
    c_values,
    raw_dt,
    step_size_bias,
    decay_rates,
    skip_gain,
    seg_ids,
    seg_before,
    rounded_inputs=None,
):
    highest = lax.Precision.HIGHEST
    step_dt = jax.nn.softplus(raw_dt + step_size_bias)
    running = jnp.cumsum(step_dt * decay_rates, axis=1)
    run_heads = jnp.swapaxes(running, 1, 2)
    length = seg_ids.shape[1]
    causal = jnp.arange(length)[:, None] >= jnp.arange(length)[None, :]
    allowed = (causal[None] & (seg_ids[:, :, None] == seg_ids[:, None, :]))[:, None]
    spread = run_heads[:, :, :, None] - run_heads[:, :, None, :]
    decay_mask = jnp.where(allowed, jnp.exp(jnp.where(allowed, spread, 0.0)), 0.0)
    if rounded_inputs is None:
        intersection = jnp.einsum("stn,sun->stu", c_values, b_values, precision=highest)
    else:
        intersection = jnp.einsum(
            "stn,sun->stu", rounded_inputs[1], rounded_inputs[0], preferred_element_type=jnp.float32
        )
    weights = decay_mask * intersection[:, None] * jnp.swapaxes(step_dt, 1, 2)[:, :, None, :]
    outputs = jnp.einsum("shtu,suhp->sthp", weights, x_heads, precision=highest)
    outputs = outputs + skip_gain[:, None] * x_heads
    linked = (seg_ids == seg_before[:, None]).astype(jnp.float32)
    reach_in = jnp.exp(running) * linked[:, :, None]
    final_log = running[:, -1, :]
    ending = (seg_ids == seg_ids[:, -1:]).astype(jnp.float32)
    toward = jnp.exp(final_log[:, None, :] - running) * ending[:, :, None] * step_dt
    local_state = jnp.einsum("sth,stn,sthp->shpn", toward, b_values, x_heads, precision=highest)
    passing = jnp.exp(final_log) * (seg_ids[:, -1] == seg_before).astype(jnp.float32)[:, None]
    return (outputs, local_state, passing, reach_in)


def carried_term(reach_in, c_values, carried):
    return reach_in[..., None] * jnp.einsum(
        "stn,shpn->sthp", c_values, carried, precision=lax.Precision.HIGHEST
    )


def chain_combine(earlier, later_part):
    return (
        earlier[0] * later_part[0],
        later_part[0][:, :, None, None] * earlier[1] + later_part[1],
    )


def per_device(
    tokens,
    output_cotangent,
    segments,
    sequence_adapter,
    input_norm_gain,
    gate_x_projection_weight,
    bc_projection_weight,
    step_projection_weight,
    x_convolution_taps,
    x_convolution_bias,
    bc_convolution_taps,
    bc_convolution_bias,
    step_size_bias,
    log_decay_rate,
    head_skip_gain,
    gated_norm_gain,
    output_projection_weight,
    in_adapter_down,
    in_adapter_up,
    out_adapter_down,
    out_adapter_up,
):
    seqs_here, block_len, unused_width = tokens.shape
    heads_here = step_projection_weight.shape[1]
    inner_here = gate_x_projection_weight.shape[2]
    head_size = inner_here // heads_here
    state_size = bc_projection_weight.shape[1] // 2
    tap_count = x_convolution_taps.shape[0]
    highest = lax.Precision.HIGHEST
    full_zx, full_bc, full_dt, full_out = gather_turned(
        (
            gate_x_projection_weight,
            bc_projection_weight,
            step_projection_weight,
            output_projection_weight,
        ),
        ("fsdp", "context"),
        (0, 0, 0, 1),
    )
    tokens_wide = tokens.astype(jnp.float32)
    scale_in = lax.rsqrt(jnp.mean(tokens_wide * tokens_wide, -1, keepdims=True) + EPS_NORM)
    normed = (tokens_wide * scale_in * input_norm_gain).astype(jnp.bfloat16)
    adapter_select = (
        sequence_adapter[:, None] == jnp.arange(in_adapter_down.shape[0], dtype=jnp.int32)[None, :]
    )
    select_rank_rows = adapter_select.astype(jnp.bfloat16)
    pick_wide = adapter_select.astype(jnp.float32)
    down_in = jnp.einsum(
        "vn,nuc->vuc", select_rank_rows, in_adapter_down, preferred_element_type=jnp.float32
    ).astype(jnp.bfloat16)
    up_in = jnp.einsum(
        "yh,hjdz->yjdz", select_rank_rows, in_adapter_up, preferred_element_type=jnp.float32
    ).astype(jnp.bfloat16)
    down_out = jnp.einsum(
        "qd,dzy->qzy", select_rank_rows, out_adapter_down, preferred_element_type=jnp.float32
    ).astype(jnp.bfloat16)
    up_out = jnp.einsum(
        "nw,wiy->niy", select_rank_rows, out_adapter_up, preferred_element_type=jnp.float32
    ).astype(jnp.bfloat16)
    low_rank = jnp.einsum(
        "std,sdr->str", normed, down_in, preferred_element_type=jnp.float32
    ).astype(jnp.bfloat16)
    gate_x = (
        jnp.einsum("std,dkc->stkc", normed, full_zx, preferred_element_type=jnp.float32)
        + jnp.einsum("str,srkc->stkc", low_rank, up_in, preferred_element_type=jnp.float32)
    ).astype(jnp.bfloat16)
    bc_proj = jnp.einsum("std,dn->stn", normed, full_bc, preferred_element_type=jnp.float32).astype(
        jnp.bfloat16
    )
    raw_dt = jnp.einsum("std,dh->sth", normed, full_dt, preferred_element_type=jnp.float32).astype(
        jnp.bfloat16
    )
    conv_in = jnp.concatenate([gate_x[:, :, 1], bc_proj], -1)
    tail_ids = (segments[:, block_len - tap_count + 1 :] + 1).astype(jnp.bfloat16)
    edge_rows, edge_ids = from_behind(
        (conv_in[:, block_len - tap_count + 1 :], tail_ids), "context", 1
    )
    before_ids = edge_ids.astype(jnp.int32) - 1
    padded = jnp.concatenate([edge_rows, conv_in], 1).astype(jnp.float32)
    padded_seg = jnp.concatenate([before_ids, segments], 1)
    seg_before = before_ids[:, -1]
    tap_weight = jnp.concatenate([x_convolution_taps, bc_convolution_taps], 1)
    tap_bias = jnp.concatenate([x_convolution_bias, bc_convolution_bias], 0)
    conv_out = conv_silu(padded, padded_seg, segments, tap_weight, tap_bias)
    x_conv = conv_out[..., :inner_here].astype(jnp.bfloat16)
    b_conv = conv_out[..., inner_here : inner_here + state_size].astype(jnp.bfloat16)
    c_conv = conv_out[..., inner_here + state_size :].astype(jnp.bfloat16)
    x_heads = x_conv.astype(jnp.float32).reshape(seqs_here, block_len, heads_here, head_size)
    b_wide = b_conv.astype(jnp.float32)
    c_wide = c_conv.astype(jnp.float32)
    dt_wide = raw_dt.astype(jnp.float32)
    decay_rates = -jnp.exp(log_decay_rate)
    outputs_local, local_state, passing, reach_in = ssd_parts(
        x_heads,
        b_wide,
        c_wide,
        dt_wide,
        step_size_bias,
        decay_rates,
        head_skip_gain,
        segments,
        seg_before,
        (b_conv, c_conv),
    )
    carry_result = carried_in(
        (passing, local_state),
        "context",
        chain_combine,
        (jnp.ones_like(passing), jnp.zeros_like(local_state)),
    )
    state_in = carry_result[1]
    ssd_out = (outputs_local + carried_term(reach_in, c_wide, state_in)).reshape(
        seqs_here, block_len, inner_here
    )
    z_vals = gate_x[:, :, 0].astype(jnp.float32)
    gate_sig = jax.nn.sigmoid(z_vals)
    gated_mix = ssd_out * z_vals * gate_sig
    square_sum = of_everyone(jnp.sum(gated_mix * gated_mix, -1), "tensor")
    scale_gate = lax.rsqrt(square_sum[..., None] / INNER_CHANNELS + EPS_NORM)
    gate_normed = (gated_mix * scale_gate * gated_norm_gain).astype(jnp.bfloat16)
    low_out = of_everyone(
        jnp.einsum("stc,scr->str", gate_normed, down_out, preferred_element_type=jnp.float32),
        "tensor",
    ).astype(jnp.bfloat16)
    partial_out = jnp.einsum(
        "stc,cd->std", gate_normed, full_out, preferred_element_type=jnp.float32
    )
    share_len = block_len // lax.axis_size("tensor")
    share_start = lax.axis_index("tensor") * share_len
    branch_share = summed_on_arrival(partial_out, "tensor", 1)
    tokens_share = lax.dynamic_slice_in_dim(tokens_wide, share_start, share_len, 1)
    low_share = lax.dynamic_slice_in_dim(low_out, share_start, share_len, 1)
    branch_share = branch_share + jnp.einsum(
        "str,srd->std", low_share, up_out, preferred_element_type=jnp.float32
    )
    out_share = (tokens_share + branch_share).astype(jnp.bfloat16)
    layer_out = lax.all_gather(out_share, "tensor", axis=1, tiled=True)
    back_zx, back_bc, back_dt, back_out = (full_zx, full_bc, full_dt, full_out)
    d_low = jnp.einsum(
        "std,srd->str", output_cotangent, up_out, preferred_element_type=jnp.float32
    ).astype(jnp.bfloat16)
    grad_up_out = jnp.einsum(
        "str,std->srd", low_out, output_cotangent, preferred_element_type=jnp.float32
    )
    d_normed = jnp.einsum(
        "std,cd->stc", output_cotangent, back_out, preferred_element_type=jnp.float32
    ) + jnp.einsum("str,scr->stc", d_low, down_out, preferred_element_type=jnp.float32)
    grad_down_out = jnp.einsum(
        "stc,str->scr", gate_normed, d_low, preferred_element_type=jnp.float32
    )
    pulled = d_normed * gated_norm_gain
    norm_dot = of_everyone(jnp.sum(pulled * gated_mix, -1), "tensor")
    d_gated = scale_gate * pulled - gated_mix * scale_gate**3 * norm_dot[..., None] / INNER_CHANNELS
    d_ssd = d_gated * z_vals * gate_sig
    d_z = d_gated * ssd_out * gate_sig * (1.0 + z_vals * (1.0 - gate_sig))
    d_heads = d_ssd.reshape(seqs_here, block_len, heads_here, head_size)

    def ssd_whole(heads_in, b_in, c_in, dt_in):
        out_local, loc_state, pass_decay, reach_part = ssd_parts(
            heads_in,
            b_in,
            c_in,
            dt_in,
            step_size_bias,
            decay_rates,
            head_skip_gain,
            segments,
            seg_before,
        )
        return (
            out_local + carried_term(reach_part, c_in, state_in),
            loc_state,
            pass_decay,
            reach_part,
        )

    unused_primal, ssd_pull = jax.vjp(ssd_whole, x_heads, b_wide, c_wide, dt_wide)
    pull_state = jnp.einsum("sth,stn,sthp->shpn", reach_in, c_wide, d_heads, precision=highest)
    later_result = entering(
        (passing, pull_state),
        "context",
        chain_combine,
        (jnp.ones_like(passing), jnp.zeros_like(pull_state)),
    )
    later_grads = later_result[1]
    d_passing = jnp.sum(later_grads * state_in, axis=(2, 3))
    dx_heads, d_b, d_c, d_dt = ssd_pull((d_heads, later_grads, d_passing, jnp.zeros_like(reach_in)))
    conv_cot = jnp.concatenate([dx_heads.reshape(seqs_here, block_len, inner_here), d_b, d_c], -1)
    unused_conv, conv_pull = jax.vjp(
        lambda padded_rows: conv_silu(padded_rows, padded_seg, segments, tap_weight, tap_bias),
        padded,
    )
    d_padded = conv_pull(conv_cot)[0]
    edge_back = from_behind(
        d_padded[:, : tap_count - 1].astype(jnp.bfloat16), "context", -1
    ).astype(jnp.float32)
    d_conv_in = d_padded[:, tap_count - 1 :] + jnp.pad(
        edge_back, ((0, 0), (block_len - tap_count + 1, 0), (0, 0))
    )
    d_gate_x = jnp.stack([d_z, d_conv_in[..., :inner_here]], 2).astype(jnp.bfloat16)
    d_dt_low = d_dt.astype(jnp.bfloat16)
    rank_part = jnp.einsum("stkc,srkc->str", d_gate_x, up_in, preferred_element_type=jnp.float32)
    bc_sum, rank_sum = (
        of_everyone(d_conv_in[..., inner_here:], "tensor"),
        of_everyone(rank_part, "tensor"),
    )
    d_bc = bc_sum.astype(jnp.bfloat16)
    d_rank = rank_sum.astype(jnp.bfloat16)
    grad_up_in = jnp.einsum(
        "str,stkc->srkc", low_rank, d_gate_x, preferred_element_type=jnp.float32
    )
    grad_down_in = jnp.einsum("std,str->sdr", normed, d_rank, preferred_element_type=jnp.float32)
    head_part = jnp.einsum(
        "stkc,dkc->std", d_gate_x, back_zx, preferred_element_type=jnp.float32
    ) + jnp.einsum("sth,dh->std", d_dt_low, back_dt, preferred_element_type=jnp.float32)
    d_in = (
        lax.psum(head_part.astype(jnp.bfloat16), "tensor").astype(jnp.float32)
        + jnp.einsum("stn,dn->std", d_bc, back_bc, preferred_element_type=jnp.float32)
        + jnp.einsum("str,sdr->std", d_rank, down_in, preferred_element_type=jnp.float32)
    )
    pulled_in = d_in * input_norm_gain
    grad_tokens = (
        scale_in * pulled_in
        - tokens_wide * scale_in**3 * jnp.mean(pulled_in * tokens_wide, -1, keepdims=True)
        + output_cotangent.astype(jnp.float32)
    )
    table_in_a = jnp.einsum("sa,sdr->adr", pick_wide, grad_down_in, precision=highest)
    table_in_b = jnp.einsum("sa,srkc->arkc", pick_wide, grad_up_in, precision=highest)
    table_out_a = jnp.einsum("sa,scr->acr", pick_wide, grad_down_out, precision=highest)
    table_out_b = jnp.einsum("sa,srd->ard", pick_wide, grad_up_out, precision=highest)
    adapter_sums = lax.psum((table_in_a, table_in_b, table_out_a, table_out_b), ("fsdp", "context"))
    return (
        layer_out,
        grad_tokens,
        adapter_sums[0],
        adapter_sums[1],
        adapter_sums[2],
        adapter_sums[3],
    )


def solution(mesh):
    placed = (
        P("fsdp", "context", None),
        P("fsdp", "context", None),
        P("fsdp", "context"),
        P("fsdp"),
        P(),
        P(("fsdp", "context"), None, "tensor"),
        P(("fsdp", "context"), None),
        P(("fsdp", "context"), "tensor"),
        P(None, "tensor"),
        P("tensor"),
        P(),
        P(),
        P("tensor"),
        P("tensor"),
        P("tensor"),
        P("tensor"),
        P("tensor", ("fsdp", "context")),
        P(),
        P(None, None, None, "tensor"),
        P(None, "tensor", None),
        P(),
    )
    return jax.shard_map(
        per_device,
        mesh=mesh,
        in_specs=placed,
        out_specs=(
            P("fsdp", "context", None),
            P("fsdp", "context", None),
            P(),
            P(None, None, None, "tensor"),
            P(None, "tensor", None),
            P(),
        ),
        check_vma=False,
    )
```

profile of v0, /device:TPU:0, one launch (start us, length us, event | category | flops | bytes accessed | tf_op | source)
XLA Modules:
  0.0 667.4 jit_solution(12924821072244629913)
XLA Ops:
  30.6 36.4 %all-gather.7.cloned.1.call-done = bf16[1536,2572]{1,0:T(8,128)(2,1)} async-done(((bf16[48,2572]{1,0:T(8,128)(2,1)}), bf16[1536,2572]{1,0:T(8,128)(2,1)}) %all-gather.7.cloned.1.call-update) | async-done | bytes 7901200 | tf_op jit(solution)/shard_map/all_gather | solution.py:16
  78.0 5.0 split.16
  82.9 6.6 copy.447
  89.6 7.0 %fusion.39 = f32[4,256,2,768]{3,1,2,0:T(8,128)S(1)} fusion(bf16[1536,2,768,1]{0,2,1,3:T(8,128)(2,1)} %bitcast.273, bf16[4,256,1536]{2,1,0:T(8,128)(2,1)S(1)} %copy-done.2, f32[1536]{0:T(1024)S(1)} %copy-done.101, f32[4,256]{1,0:T(4,128)S(1)} %copy-done.91), kind=kOutput, calls=%fused_computation.71 | convolution fusion | flops 4838129664 | bytes 14166016 | tf_op jit(solution)/shard_map/std,dkc->stkc/dot_general | solution.py:226
  136.4 10.4 %all_gather.31 = bf16[4,4,12]{2,1,0:T(4,128)(2,1)} all-gather(bf16[1,4,12]{2,1,0:T(4,128)(2,1)S(1)} %get-tuple-element.270), channel_id=1, replica_groups=mesh['fsdp'=8,'context'=4,'tensor'=4] {'context'}, dimensions={0}, use_global_device_ids=true | all-gather | bytes 480 | tf_op jit(solution)/shard_map/all_gather | solution.py:77
  146.9 10.8 %all_gather.27 = f32[4,4,12]{2,1,0:T(4,128)S(1)} all-gather(f32[1,4,12]{2,1,0:T(4,128)S(1)} %get-tuple-element.271), channel_id=1, replica_groups=mesh['fsdp'=8,'context'=4,'tensor'=4] {'context'}, dimensions={0}, use_global_device_ids=true | all-gather | bytes 960 | tf_op jit(solution)/shard_map/all_gather | solution.py:34
  157.6 7.4 %fusion.59 = f32[768,4,256]{0,2,1:T(8,128)} fusion(bf16[4,256,1536]{2,1,0:T(8,128)(2,1)} %param.26, bf16[1536,2572]{1,0:T(8,128)(2,1)} %all-gather.7.cloned.1.call-done), kind=kOutput, calls=%fused_computation.104 | convolution fusion | flops 2415919104 | bytes 8650752 | tf_op jit(solution)/shard_map/std,cd->stc/dot_general | solution.py:307
  167.6 20.0 %all-gather.11.cloned.1.call-done = f32[16,12,64,128]{3,2,1,0:T(8,128)} async-done(((f32[4,12,64,128]{3,2,1,0:T(8,128)}), f32[16,12,64,128]{3,2,1,0:T(8,128)}) %all-gather.11.cloned.1.call-update) | async-done | bytes 6291472 | tf_op jit(solution)/shard_map/all_gather | solution.py:34
  187.6 7.2 %while.29 = (s32[]{:T(128)}, f32[4,12,64,128]{3,2,1,0:T(8,128)S(1)}, s32[]{:T(128)}, f32[4,4,12]{2,1,0:T(4,128)S(1)}, f32[4,4,12,64,128]{4,3,2,1,0:T(8,128)}, /*index=5*/s32[]{:T(128)}, s32[]{:T(128)}) while((s32[]{:T(128)}, f32[4,12,64,128]{3,2,1,0:T(8,128)S(1)}, s32[]{:T(128)}, f32[4,4,12]{2,1,0:T(4,128)S(1)}, ...), condition=%wide.region_4.5_spmd.clone, body=%wide.region_3.4_spmd.clone.sunk | while | flops 1572868 | bytes 4719281 | solution.py:46
  197.5 12.1 %multiply_reduce_fusion.6 = (f32[4,256]{1,0:T(4,128)S(1)}, f32[4,256,12,64]{1,3,2,0:T(8,128)}) fusion(f32[4,256,12,64]{1,3,2,0:T(8,128)S(1)} %bitcast.275, f32[4,256,12,64]{1,3,2,0:T(8,128)S(1)} %fusion.107, f32[4,256,12]{1,2,0:T(8,128)S(1)} %copy.362, bf16[4,256,12,64]{1,3,2,0:T(8,128)(2,1)S(1)} %bitcast.262, f32[12]{0:T(128)S(1)} %copy-done.107, ...), kind=kOutput, calls=%fused_computation.95 | convolution fusion | flops 2441083904 | bytes 12472368 | tf_op jit(solution)/shard_map/shtu,suhp->sthp/dot_general | solution.py:137
  218.1 7.3 %multiply_reduce_fusion.5 = (f32[4,256]{1,0:T(4,128)S(1)}, f32[4,256,768]{2,1,0:T(8,128)}, f32[4,256,768]{2,1,0:T(8,128)}) fusion(f32[4,256,768]{2,1,0:T(8,128)} %copy.368, bf16[4,256,2,768]{3,1,2,0:T(8,128)(2,1)} %copy-done.11, f32[768]{0:T(1024)S(1)} %copy-done.86, bf16[4,16,256]{2,1,0:T(8,128)(2,1)S(1)} %convolution_convert_fusion.5, ...), kind=kOutput, calls=%fused_computation.92 | convolution fusion | flops 33029120 | bytes 14294016 | tf_op jit(solution)/shard_map/str,scr->stc/dot_general | solution.py:309
  225.5 6.4 reshape.316
  231.8 6.7 %copy.365 = f32[4,4,64,768]{3,2,1,0:T(8,128)} copy(f32[4,4,64,768]{2,1,3,0:T(4,128)} %reshape.316) | data formatting | bytes 6291456 | tf_op jit(solution)/shard_map/reshape | solution.py:274
  239.2 5.0 all-to-all-start.3
  249.5 6.7 %fusion.75 = (bf16[4,256,1,768]{3,1,0,2:T(8,128)(2,1)}, f32[4,256,768]{2,1,0:T(8,128)}) fusion(f32[4,256,768]{2,1,0:T(8,128)} %copy.368, bf16[4,256,2,768]{3,1,2,0:T(8,128)(2,1)} %copy-done.11, f32[4,256]{1,0:T(4,128)S(1)} %reduce_sum.185, f32[4,256,768]{2,1,0:T(8,128)} %get-tuple-element.273, f32[4,256]{1,0:T(4,128)S(1)} %get-tuple-element.296, ...), kind=kLoop, calls=%fused_computation.122 | loop fusion | flops 14155776 | bytes 15740928 | tf_op jit(solution)/shard_map/stack | solution.py:362
  275.8 17.2 %fusion.11 = (f32[4,12,256]{2,1,0:T(8,128)}, f32[4,12,256]{2,1,0:T(8,128)}, f32[4,12,256]{2,1,0:T(8,128)}, f32[4,256,256]{2,1,0:T(8,128)}) fusion(f32[4,256,256]{2,1,0:T(8,128)} %fusion.124, f32[4,12,256]{2,1,0:T(8,128)} %copy-done.62, f32[4,12,256]{2,1,0:T(8,128)} %copy.357, pred[4,256,256]{2,1,0:T(8,128)(4,1)} %compare_and_fusion, ...), kind=kOutput, calls=%fused_computation.17 | convolution fusion | flops 2462806016 | bytes 7323648 | tf_op jit(solution)/shard_map/transpose(jvp(shtu,suhp->sthp))/dot_general | solution.py:137
  298.7 7.2 %convolution_bitcast_fusion = f32[4,4,64,1536]{3,2,0,1:T(8,128)S(1)} fusion(bf16[1536,2572]{1,0:T(8,128)(2,1)} %all-gather.7.cloned.1.call-done, f32[4,4,64,768]{3,2,1,0:T(8,128)} %bitcast.269, f32[4,4,64,768]{3,2,1,0:T(8,128)} %copy.365, f32[768]{0:T(1024)S(1)} %copy-done.87, f32[4,4,64]{2,1,0:T(4,128)} %rsqrt.28), kind=kOutput, calls=%fused_computation.43 | convolution fusion | flops 2422210560 | bytes 14953472 | tf_op jit(solution)/shard_map/stc,cd->std/dot_general | solution.py:287
  309.1 5.1 fusion.80
  322.7 7.0 %while.28 = (s32[]{:T(128)}, f32[4,12,64,128]{3,2,1,0:T(8,128)S(1)}, s32[]{:T(128)}, bf16[4,4,12]{2,1,0:T(4,128)(2,1)}, bf16[4,4,12,64,128]{4,3,2,1,0:T(8,128)(2...) while((s32[]{:T(128)}, f32[4,12,64,128]{3,2,1,0:T(8,128)S(1)}, s32[]{:T(128)}, ...), condition=%wide.region_12.13_spmd, body=%wide.region_11.12_spmd.sunk | while | flops 1179702 | bytes 3932795 | solution.py:94
  331.1 5.2 fusion.79
  341.3 12.8 %bitcast_add_fusion.2 = f32[4,256,12,64]{1,3,2,0:T(8,128)} fusion(f32[4,256,12,64]{1,3,2,0:T(8,128)S(1)} %bitcast.259, f32[4,256,12,64]{1,3,2,0:T(8,128)S(1)} %get-tuple-element.304, f32[4,12,64,256]{3,2,1,0:T(8,128)S(1)} %bitcast.260, f32[4,256,256]{2,1,0:T(8,128)S(1)} %copy-done.42, f32[4,12,256]{2,1,0:T(8,128)S(1)} %copy-done.63, ...), kind=kOutput, calls=%fused_computation.73 | convolution fusion | flops 2434793472 | bytes 14041136 | tf_op jit(solution)/shard_map/transpose(jvp(shtu,suhp->sthp))/dot_general | solution.py:137
  363.4 9.9 %reduce-window.16 = f32[4,12,2,128]{3,1,2,0:T(8,128)S(1)} reduce-window(f32[4,12,2,128]{3,1,2,0:T(8,128)S(1)} %copy.393, f32[]{:T(128)} %constant.104.clone.1), window={size=1x1x1x128 pad=0_0x0_0x0_0x0_127}, to_apply=%region_20.21 | reduce-window | flops 1560576 | bytes 98308 | tf_op jit(solution)/shard_map/reduce-window.2
  382.3 6.1 pad_add_fusion
  415.6 5.2 all-to-all-start.1
  428.0 7.9 %fusion.170 = f32[4,256,1536,1]{2,1,0,3:T(8,128)S(1)} fusion(bf16[1536,2,768,1]{0,2,3,1:T(8,128)(2,1)} %bitcast.274, bf16[4,256,1,768]{3,1,0,2:T(8,128)(2,1)} %copy-done.39, bf16[4,256,1,768]{3,1,0,2:T(8,128)(2,1)} %get-tuple-element.278), kind=kOutput, calls=%fused_computation.266 | convolution fusion | flops 4833411072 | bytes 14155776 | tf_op jit(solution)/shard_map/stkc,dkc->std/dot_general | solution.py:375
  441.9 45.7 %all-to-all-done.1 = f32[4,4,64,1536]{3,2,1,0:T(8,128)} async-done(((f32[4,4,64,1536]{3,2,1,0:T(8,128)}), f32[4,4,64,1536]{3,2,1,0:T(8,128)}, u32[]{:S(2)}, u32[]{:S(2)}) %all-to-all-start.1) | async-done | bytes 6291488 | tf_op jit(solution)/shard_map/all_to_all | solution.py:68
  491.2 4.8 all-to-all-start.4
  508.2 29.1 %all-reduce.12.cloned.1.call-done = (f32[8,1536,16]{1,0,2:T(8,128)}, f32[8,16,2,768]{3,0,2,1:T(8,128)}, f32[8,768,16]{1,0,2:T(8,128)}, f32[8,16,1536]{2,0,1:T(8,128)}) async-done(((f32[8,1536,16]{1,0,2:T(8,128)}, f32[8,16,2,768]{3,0,2,1:T(8,128)}, f32[8,768,16]{1,0,2:T(8,128)}, f32[8,16,1536]{2,0,1:T(8,128)}), (f32[8,1536,16]{1,0,2:T(8,128)}, f32[8,16,2,768]{3,0,2,1:T(8,128)}, f32[8,768,16]{1,0,2:T(8,128)}, ...) | async-done | bytes 2752528 | tf_op jit(solution)/shard_map/psum | solution.py:393
  548.9 5.0 fusion.84
  554.0 61.4 %all-reduce.10.cloned.1.call-done = bf16[4,256,1536]{2,1,0:T(8,128)(2,1)} async-done(((bf16[4,256,1536]{2,1,0:T(8,128)(2,1)}), bf16[4,256,1536]{2,1,0:T(8,128)(2,1)}) %all-reduce.10.cloned.1.call-update) | async-done | bytes 3145744 | tf_op jit(solution)/shard_map/psum | solution.py:379
  615.4 5.6 multiply_reduce_fusion.2
  624.7 31.7 %all-gather.9.cloned.1.call-done = bf16[4,256,1536]{2,1,0:T(8,128)(2,1)} async-done(((bf16[4,64,1536]{2,1,0:T(8,128)(2,1)}), bf16[4,256,1536]{2,1,0:T(8,128)(2,1)}) %all-gather.9.cloned.1.call-update) | async-done | bytes 3145744 | tf_op jit(solution)/shard_map/all_gather | solution.py:299
  (387 shorter events, 242.9 us)
Async XLA Ops:
  7.2 17.9 %copy-start = (bf16[8,1536,16]{1,2,0:T(8,128)(2,1)S(1)}, bf16[8,1536,16]{1,2,0:T(8,128)(2,1)}, u32[]{:S(2)}) copy-start(bf16[8,1536,16]{1,2,0:T(8,128)(2,1)} %param.42) | copy-start | bytes 1179652
  7.2 19.3 %copy-start.2 = (bf16[4,256,1536]{2,1,0:T(8,128)(2,1)S(1)}, bf16[4,256,1536]{2,1,0:T(8,128)(2,1)}, u32[]{:S(2)}) copy-start(bf16[4,256,1536]{2,1,0:T(8,128)(2,1)} %param.25) | copy-start | bytes 9437188
  7.2 17.8 %copy-start.82 = (s32[4]{0:T(128)S(1)}, s32[4]{0:T(128)}, u32[]{:S(2)}) copy-start(s32[4]{0:T(128)} %param.28) | copy-start | bytes 52
  7.2 59.8 %all-gather.7.cloned.1.call-start = ((), (), s32[]{:S(2)}) async-start(), calls=%async_computation.6 | async-start | bytes 8515584 | tf_op jit(solution)/shard_map/all_gather | solution.py:16
  11.7 176.0 %all-gather.11.cloned.1.call-start = ((), (), s32[]{:S(2)}) async-start(), calls=%async_computation.9 | async-start | bytes 7864320 | tf_op jit(solution)/shard_map/all_gather | solution.py:34
  12.5 15.6 %collective-permute-start.1 = (bf16[4,3]{1,0:T(4,128)(2,1)S(1)}, bf16[4,3]{1,0:T(4,128)(2,1)S(1)}, u32[]{:S(2)}, u32[]{:S(2)}) collective-permute-start(bf16[4,3]{1,0:T(4,128)(2,1)S(1)} %add_convert_fusion.1), channel_id=1, source_target_pairs={{0,4},{4,8},{8,12},{1,5},{5,9},{9,13},{2,6},{6,10},{10,14},{3,7},{... | collective-permute-start | bytes 80 | tf_op jit(solution)/shard_map/ppermute | solution.py:29
  26.5 40.5 %copy-start.100 = (f32[1536]{0:T(1024)S(1)}, f32[1536]{0:T(1024)}, u32[]{:S(2)}) copy-start(f32[1536]{0:T(1024)} %param.29) | copy-start | bytes 18436
  28.1 41.2 %copy-start.80 = (s32[4,3]{1,0:T(4,128)}, s32[4,3]{1,0:T(4,128)S(1)}, u32[]{:S(2)}) copy-start(s32[4,3]{1,0:T(4,128)S(1)} %convert_add_fusion.3) | copy-start | bytes 148
  30.6 38.7 %copy-start.95 = (f32[12]{0:T(128)S(1)}, f32[12]{0:T(128)}, u32[]{:S(2)}) copy-start(f32[12]{0:T(128)} %param.37) | copy-start | bytes 148
  30.6 38.7 %copy-start.105 = (f32[12]{0:T(128)S(1)}, f32[12]{0:T(128)}, u32[]{:S(2)}) copy-start(f32[12]{0:T(128)} %exponential_negate_fusion) | copy-start | bytes 148
  103.2 5.4 collective-permute-start
  117.3 158.5 %copy-start.9 = (bf16[4,256,768]{1,2,0:T(8,128)(2,1)}, bf16[4,256,768]{1,2,0:T(8,128)(2,1)S(1)}, u32[]{:S(2)}) copy-start(bf16[4,256,768]{1,2,0:T(8,128)(2,1)S(1)} %copy.349) | copy-start | bytes 4718596
  128.4 89.7 %copy-start.59 = (bf16[4,16,256]{2,1,0:T(8,128)(2,1)}, bf16[4,16,256]{2,1,0:T(8,128)(2,1)S(1)}, u32[]{:S(2)}) copy-start(bf16[4,16,256]{2,1,0:T(8,128)(2,1)S(1)} %convolution_convert_fusion.5) | copy-start | bytes 98308
  130.5 66.9 %copy-start.62 = (f32[4,12,256]{2,1,0:T(8,128)}, f32[4,12,256]{2,1,0:T(8,128)S(1)}, u32[]{:S(2)}) copy-start(f32[4,12,256]{2,1,0:T(8,128)S(1)} %copy.359) | copy-start | bytes 147460
  210.3 28.3 %all-to-all-start = ((f32[4,4,256]{2,1,0:T(4,128)}), f32[4,4,256]{2,1,0:T(4,128)S(1)}, u32[]{:S(2)}, u32[]{:S(2)}) async-start(f32[4,4,256]{2,1,0:T(4,128)} %broadcast_in_dim.39), calls=%async_computation | async-start | bytes 32768 | tf_op jit(solution)/shard_map/all_to_all | solution.py:51
  239.2 10.3 %all-to-all-start.3 = ((f32[4,4,256]{2,1,0:T(4,128)}), f32[4,4,256]{2,1,0:T(4,128)S(1)}, u32[]{:S(2)}, u32[]{:S(2)}) async-start(f32[4,4,256]{2,1,0:T(4,128)} %broadcast_in_dim.41), calls=%async_computation.3 | async-start | bytes 32768 | tf_op jit(solution)/shard_map/all_to_all | solution.py:51
  268.3 50.0 %all-to-all-start.2 = ((f32[4,4,256,16]{2,3,1,0:T(8,128)}), f32[4,4,256,16]{2,3,1,0:T(8,128)S(1)}, u32[]{:S(2)}, u32[]{:S(2)}) async-start(f32[4,4,256,16]{2,3,1,0:T(8,128)} %broadcast_in_dim.40), calls=%async_computation.2 | async-start | bytes 524288 | tf_op jit(solution)/shard_map/all_to_all | solution.py:51
  271.7 50.8 %all-gather.13.cloned.1.call-start = ((), (), s32[]{:S(2)}) async-start(), calls=%async_computation.10 | async-start | bytes 3932160 | tf_op jit(solution)/shard_map/all_gather | solution.py:77
  275.8 22.9 %copy-start.87 = (f32[768]{0:T(1024)S(1)}, f32[768]{0:T(1024)}, u32[]{:S(2)}) copy-start(f32[768]{0:T(1024)} %param.40) | copy-start | bytes 9220
  357.8 16.4 %copy-start.33 = (f32[4,256,128]{2,1,0:T(8,128)S(1)}, f32[4,256,128]{2,1,0:T(8,128)}, u32[]{:S(2)}) copy-start(f32[4,256,128]{2,1,0:T(8,128)} %convolution_add_fusion.1) | copy-start | bytes 1572868
  357.8 16.4 %copy-start.77 = (f32[1,1024]{1,0:T(1,128)S(1)}, f32[1,1024]{1,0:T(1,128)}, u32[]{:S(2)}) copy-start(f32[1,1024]{1,0:T(1,128)} %get-tuple-element.288) | copy-start | bytes 12292
  358.1 20.3 %copy-start.25 = (f32[4,256,12]{2,0,1:T(4,128)}, f32[4,256,12]{2,0,1:T(4,128)S(1)}, u32[]{:S(2)}) copy-start(f32[4,256,12]{2,0,1:T(4,128)S(1)} %copy.432) | copy-start | bytes 147460
  390.6 5.8 collective-permute-start.2
  403.5 11.4 %all-to-all-start.5 = ((f32[4,4,256,16]{2,3,1,0:T(8,128)}), f32[4,4,256,16]{2,3,1,0:T(8,128)S(1)}, u32[]{:S(2)}, u32[]{:S(2)}) async-start(f32[4,4,256,16]{2,3,1,0:T(8,128)} %broadcast_in_dim.43), calls=%async_computation.5 | async-start | bytes 524288 | tf_op jit(solution)/shard_map/all_to_all | solution.py:51
  415.6 72.0 %all-to-all-start.1 = ((f32[4,4,64,1536]{3,2,1,0:T(8,128)}), f32[4,4,64,1536]{3,2,1,0:T(8,128)}, u32[]{:S(2)}, u32[]{:S(2)}) async-start(f32[4,4,64,1536]{3,2,1,0:T(8,128)} %copy.367), calls=%async_computation.1 | async-start | bytes 12582912 | tf_op jit(solution)/shard_map/all_to_all | solution.py:68
  420.9 116.3 %all-reduce.12.cloned.1.call-start = ((), (), s32[]{:S(2)}) async-start(), calls=%async_computation.11 | async-start | bytes 5505024 | tf_op jit(solution)/shard_map/psum | solution.py:393
  427.9 187.4 %all-reduce.10.cloned.1.call-start = ((), (), s32[]{:S(2)}) async-start(), calls=%async_computation.8 | async-start | bytes 6291456 | tf_op jit(solution)/shard_map/psum | solution.py:379
  491.2 54.2 %all-to-all-start.4 = ((f32[4,4,256,256]{3,2,1,0:T(8,128)}), f32[4,4,256,256]{3,2,1,0:T(8,128)}, u32[]{:S(2)}, u32[]{:S(2)}) async-start(f32[4,4,256,256]{3,2,1,0:T(8,128)} %broadcast_in_dim.42), calls=%async_computation.4 | async-start | bytes 8388608 | tf_op jit(solution)/shard_map/all_to_all | solution.py:51
  496.1 160.3 %all-gather.9.cloned.1.call-start = ((), (), s32[]{:S(2)}) async-start(), calls=%async_computation.7 | async-start | bytes 3932160 | tf_op jit(solution)/shard_map/all_gather | solution.py:299
  548.9 66.5 %copy-start.47 = (bf16[4,1536,16]{1,0,2:T(4,128)(2,1)S(1)}, bf16[4,1536,16]{1,0,2:T(4,128)(2,1)}, u32[]{:S(2)}) copy-start(bf16[4,1536,16]{1,0,2:T(4,128)(2,1)} %copy-done.46) | copy-start | bytes 589828
  554.0 67.1 %copy-start.89 = (f32[4,256]{1,0:T(4,128)S(1)}, f32[4,256]{1,0:T(4,128)}, u32[]{:S(2)}) copy-start(f32[4,256]{1,0:T(4,128)} %get-tuple-element.294) | copy-start | bytes 12292
  621.0 39.1 %copy-start.1 = (bf16[8,1536,16]{1,2,0:T(8,128)(2,1)S(1)}, bf16[8,1536,16]{1,2,0:T(8,128)(2,1)}, u32[]{:S(2)}) copy-start(bf16[8,1536,16]{1,2,0:T(8,128)(2,1)} %param.42) | copy-start | bytes 1179652
  (92 other events, 453.2 us)
Sparse Core Ops, SparseCore 0:
  11.8 55.1 all-gather.6
  121.5 66.1 all-gather.10
  274.8 40.5 all-gather.12
  428.0 109.1 all-reduce.11
  540.2 75.1 all-reduce.9
  617.0 39.3 all-gather.8
where the time goes:
time: 678 us; the launch traced here: 667 us
  waiting for transfers between devices  236 us (35%)
  matrix products  157 us (23%)
  local copies, waits for them, and re-layouts  101 us (15%)
  other arithmetic  98.4 us (15%)
  starting transfers between devices  36.8 us (5%)
  blocking collectives  21.2 us (3%)
  between operations  16 us (2%)
    psum x1, waiting for transfers between devices, per_device(): lax.psum(head_part.astype(jnp.bfloat16), 'tensor').astype(jnp.float32)  61.4 us
    all_to_all x1, waiting for transfers between devices, summed_on_arrival(): pieces = lax.all_to_all(split_up(value, dim, size), axis, 0, 0, tiled=True)  45.7 us
    dot_general x3, matrix products, ssd_parts(): outputs = jnp.einsum('shtu,suhp->sthp', weights, x_heads, precision=highest)  42.2 us
    all_gather x1, waiting for transfers between devices, gather_turned(): filled = lax.all_gather(both, axis, axis=0, tiled=True)  36.4 us
    all_gather x1, waiting for transfers between devices, per_device(): layer_out = lax.all_gather(out_share, 'tensor', axis=1, tiled=True)  31.7 us
    unnamed x227, local copies, waits for them, and re-layouts  31 us
    psum x1, waiting for transfers between devices, per_device(): lax.psum((table_in_a, table_in_b, table_out_a, table_out_b), ('fsdp', 'co...  29.1 us
    all_to_all x5, starting transfers between devices, sent_to_all(): lax.all_to_all(jnp.broadcast_to(value[None], (size, *value.shape)), axis,...  22.2 us
  transfers between devices with their start and end apart: 15, of which 9 were waited for; matrix products, arithmetic and copies ran while one was open for 27% of the time, Pallas kernels for 0%

commit v1 on v0

v1 whole, which is shorter than its diff:
```python
import functools

import jax
import jax.numpy as jnp
from jax import lax
from jax.experimental import pallas as pl
from jax.experimental.pallas import tpu as pltpu
from jax.sharding import PartitionSpec as P

INNER_CHANNELS = 3072
EPS_NORM = 1e-05
SUB = 128
NEG = -1e30
BF = jnp.bfloat16
F32 = jnp.float32
HIGHEST = lax.Precision.HIGHEST


def dot_nn(a, b):
    return lax.dot_general(a, b, (((1,), (0,)), ((), ())), preferred_element_type=F32)


def dot_nt(a, b):
    return lax.dot_general(a, b, (((1,), (1,)), ((), ())), preferred_element_type=F32)


def dot_tn(a, b):
    return lax.dot_general(a, b, (((0,), (0,)), ((), ())), preferred_element_type=F32)


def softplus(v):
    return jnp.maximum(v, 0.0) + jnp.log1p(jnp.exp(-jnp.abs(v)))


def lane(shape, dim):
    return lax.broadcasted_iota(jnp.int32, shape, dim)


def wide(column):
    return jnp.broadcast_to(column, (SUB, SUB))


def decays(raw, par_ref):
    rate = par_ref[1:2, :]
    shifted = raw + par_ref[0:1, :]
    dt = softplus(shifted)
    lower = (lane((SUB, SUB), 0) >= lane((SUB, SUB), 1)).astype(F32)
    run = jnp.dot(lower, dt * rate, precision=HIGHEST, preferred_element_type=F32)
    return shifted, dt, rate, run


def scan_forward(
    z_ref, x_ref, bcdt_ref, marks_ref, taps_ref, bias_ref, par_ref, skip_ref, gain_ref,
    y_ref, xc_ref, bc_ref, slope_ref, g2_ref, states_ref, square_ref,
    state, ext,
):
    step = pl.program_id(0)
    inner = z_ref.shape[1]
    chans = ext.shape[1]

    @pl.when(step == 0)
    def _():
        state[...] = jnp.zeros_like(state)
        ext[0:8, :] = jnp.zeros((8, chans), F32)

    @pl.when(step > 0)
    def _():
        ext[0:8, :] = ext[SUB : SUB + 8, :]

    ext[8 : SUB + 8, 0:inner] = x_ref[...].astype(F32)
    ext[8 : SUB + 8, inner:chans] = bcdt_ref[:, 0 : 2 * SUB].astype(F32)
    near = [wide(marks_ref[:, k : k + 1]) for k in range(3)]
    linked = wide(marks_ref[:, 3:4])
    ending = wide(marks_ref[:, 4:5])
    ids = wide(marks_ref[:, 5:6])
    passing = marks_ref[0:1, 6:7]
    left = lane((SUB, SUB), 1) < 64

    def conv(sl):
        pre = bias_ref[:, sl] + taps_ref[3:4, sl] * ext[8 : SUB + 8, sl]
        for k in range(1, 4):
            pre = pre + taps_ref[3 - k : 4 - k, sl] * (ext[8 - k : SUB + 8 - k, sl] * near[k - 1])
        sig = jax.nn.sigmoid(pre)
        out = (pre * sig).astype(BF)
        slope_ref[:, sl] = (sig * (1.0 + pre * (1.0 - sig))).astype(BF)
        return out

    b_low = conv(slice(inner, inner + SUB))
    c_low = conv(slice(inner + SUB, inner + 2 * SUB))
    bc_ref[:, 0:SUB] = b_low
    bc_ref[:, SUB : 2 * SUB] = c_low
    b_turned = b_low.astype(F32).T.astype(BF)
    _, dt, _, run = decays(bcdt_ref[:, 2 * SUB : 3 * SUB].astype(F32), par_ref)
    run_rows = run.T
    allowed = (ids == ids.T) & (lane((SUB, SUB), 0) >= lane((SUB, SUB), 1))
    mask = jnp.where(allowed, 0.0, NEG)
    cross = dot_nt(c_low, b_low)
    square = jnp.zeros((SUB, SUB), F32)
    for p in range(inner // SUB):
        sl = slice(p * SUB, (p + 1) * SUB)
        x_low = conv(sl)
        xc_ref[:, sl] = x_low
        x = x_low.astype(F32)
        run0, run1 = wide(run[:, 2 * p : 2 * p + 1]), wide(run[:, 2 * p + 1 : 2 * p + 2])
        run_p = jnp.where(left, run0, run1)
        dt_p = jnp.where(left, wide(dt[:, 2 * p : 2 * p + 1]), wide(dt[:, 2 * p + 1 : 2 * p + 2]))
        m0 = (jnp.exp(run0 - run_rows[2 * p : 2 * p + 1, :] + mask) * cross).astype(BF)
        m1 = (jnp.exp(run1 - run_rows[2 * p + 1 : 2 * p + 2, :] + mask) * cross).astype(BF)
        xdt = x * dt_p
        split = jnp.concatenate([jnp.where(left, xdt, 0.0), jnp.where(left, 0.0, xdt)], 0).astype(BF)
        before = state[:, sl]
        before_low = before.astype(BF)
        states_ref[0, :, sl] = before_low
        y = dot_nn(jnp.concatenate([m0, m1], 1), split)
        y = y + jnp.exp(run_p) * linked * dot_nn(c_low, before_low) + skip_ref[:, sl] * x
        last = run_p[SUB - 1 : SUB, :]
        toward = (xdt * (jnp.exp(last - run_p) * ending)).astype(BF)
        state[:, sl] = (jnp.exp(last) * passing) * before + dot_nn(b_turned, toward)
        z = z_ref[:, sl].astype(F32)
        gated = y * (z * jax.nn.sigmoid(z))
        y_ref[:, sl] = y.astype(BF)
        g2_ref[:, sl] = (gated * gain_ref[:, sl]).astype(BF)
        square = square + gated * gated
    square_ref[...] = square


def scan_backward(
    z_ref, dt_ref, xc_ref, bc_ref, slope_ref, y_ref, dn_ref, states_ref, scale_ref, marks_ref,
    taps_ref, par_ref, skip_ref, gain_ref, pick_ref,
    da_ref,
    lam, ext, to_dt, to_run, to_end,
):
    step = pl.program_id(0)
    inner = z_ref.shape[1]
    chans = ext.shape[1]

    @pl.when(step == 0)
    def _():
        lam[...] = jnp.zeros_like(lam)
        ext[SUB : SUB + 8, :] = jnp.zeros((8, chans), F32)

    @pl.when(step > 0)
    def _():
        ext[SUB : SUB + 8, :] = ext[0:8, :]

    linked = wide(marks_ref[:, 3:4])
    ending = wide(marks_ref[:, 4:5])
    ids = wide(marks_ref[:, 5:6])
    passing = marks_ref[0:1, 6:7]
    later = [wide(marks_ref[:, 7 + k : 8 + k]) for k in range(3)]
    left = lane((SUB, SUB), 1) < 64
    rn = jnp.broadcast_to(scale_ref[0:1, :], (SUB, SUB)).T
    kappa = jnp.broadcast_to(scale_ref[1:2, :], (SUB, SUB)).T
    shifted, dt, rate, run = decays(dt_ref[...].astype(F32), par_ref)
    run_rows = run.T
    b_low, c_low = bc_ref[:, 0:SUB], bc_ref[:, SUB : 2 * SUB]
    c_turned = c_low.astype(F32).T.astype(BF)
    allowed = (ids == ids.T) & (lane((SUB, SUB), 0) <= lane((SUB, SUB), 1))
    mask = jnp.where(allowed, 0.0, NEG)
    cross = dot_nt(b_low, c_low)
    d_cross = jnp.zeros((SUB, SUB), F32)
    d_b = jnp.zeros((SUB, SUB), F32)
    d_c = jnp.zeros((SUB, SUB), F32)
    for p in range(inner // SUB):
        sl = slice(p * SUB, (p + 1) * SUB)
        z = z_ref[:, sl].astype(F32)
        sig = jax.nn.sigmoid(z)
        silu = z * sig
        y = y_ref[:, sl].astype(F32)
        d_gated = rn * (dn_ref[:, sl].astype(F32) * gain_ref[:, sl]) - kappa * (y * silu)
        da_ref[:, sl] = (d_gated * y * sig * (1.0 + z * (1.0 - sig))).astype(BF)
        dy = d_gated * silu
        x = xc_ref[:, sl].astype(F32)
        run0, run1 = wide(run[:, 2 * p : 2 * p + 1]), wide(run[:, 2 * p + 1 : 2 * p + 2])
        run_p = jnp.where(left, run0, run1)
        dt_p = jnp.where(left, wide(dt[:, 2 * p : 2 * p + 1]), wide(dt[:, 2 * p + 1 : 2 * p + 2]))
        l0 = jnp.exp(run_rows[2 * p : 2 * p + 1, :] - run0 + mask)
        l1 = jnp.exp(run_rows[2 * p + 1 : 2 * p + 2, :] - run1 + mask)
        xdt = x * dt_p
        x_split = jnp.concatenate([jnp.where(left, xdt, 0.0), jnp.where(left, 0.0, xdt)], 0).astype(BF)
        dy_split = jnp.concatenate([jnp.where(left, dy, 0.0), jnp.where(left, 0.0, dy)], 0).astype(BF)
        d_m = dot_nt(x_split, dy.astype(BF))
        d_cross = d_cross + l0 * d_m[0:SUB] + l1 * d_m[SUB : 2 * SUB]
        m = jnp.concatenate([l0 * cross, l1 * cross], 1).astype(BF)
        lam_p = lam[:, sl]
        lam_low = lam_p.astype(BF)
        last = run_p[SUB - 1 : SUB, :]
        toward = jnp.exp(last - run_p) * ending
        carried = toward * dot_nn(b_low, lam_low)
        d_xt = dot_nn(m, dy_split) + carried
        skip = skip_ref[:, sl]
        ext[0:SUB, sl] = (dt_p * d_xt + skip * dy) * slope_ref[:, sl].astype(F32)
        x_dx = x * d_xt
        to_dt[:, sl] = x_dx
        to_run[:, sl] = dy * (y - skip * x) - dt_p * x_dx
        reached = (jnp.exp(run_p) * linked * dy).astype(BF)
        before_low = states_ref[0, :, sl]
        keep = jnp.exp(last) * passing
        to_end[0:1, sl] = jnp.sum(xdt * carried, 0, keepdims=True) + keep * jnp.sum(
            lam_p * before_low.astype(F32), 0, keepdims=True
        )
        d_b = d_b + dot_nt((xdt * toward).astype(BF), lam_low)
        d_c = d_c + dot_nt(reached, before_low)
        lam[:, sl] = keep * lam_p + dot_nn(c_turned, reached)
    d_cross_low = d_cross.astype(BF)
    d_b = d_b + dot_nn(d_cross_low, c_low)
    d_c = d_c + dot_nn(d_cross.T.astype(BF), b_low)
    ext[0:SUB, inner : inner + SUB] = d_b * slope_ref[:, inner : inner + SUB].astype(F32)
    ext[0:SUB, inner + SUB : chans] = d_c * slope_ref[:, inner + SUB : chans].astype(F32)

    def by_head(v):
        high = v.astype(BF)
        return dot_nn(high, pick_ref[...]) + dot_nn((v - high.astype(F32)).astype(BF), pick_ref[...])

    d_run = by_head(to_run[...])
    d_end = by_head(to_end[...])[0:1, :]
    d_run = d_run + jnp.where(lane((SUB, SUB), 0) == SUB - 1, d_end, 0.0)
    upper = (lane((SUB, SUB), 0) <= lane((SUB, SUB), 1)).astype(F32)
    d_log = jnp.dot(upper, d_run, precision=HIGHEST, preferred_element_type=F32)
    d_dt = by_head(to_dt[...]) + rate * d_log
    da_ref[:, inner + chans : inner + chans + SUB] = (d_dt * jax.nn.sigmoid(shifted)).astype(BF)
    for s in range(chans // SUB):
        sl = slice(s * SUB, (s + 1) * SUB)
        acc = taps_ref[3:4, sl] * ext[0:SUB, sl]
        for k in range(1, 4):
            acc = acc + taps_ref[3 - k : 4 - k, sl] * (ext[k : SUB + k, sl] * later[k - 1])
        da_ref[:, inner + s * SUB : inner + (s + 1) * SUB] = acc.astype(BF)


def run_forward(gx, marks, taps, bias, par, skip, gain):
    length = gx.shape[0]
    inner = skip.shape[1]
    chans = taps.shape[1]
    steps = length // SUB
    row = lambda cols, at=0: pl.BlockSpec((SUB, cols), lambda i, at=at: (i, at))
    whole = lambda a: pl.BlockSpec(a.shape, lambda i: (0,) * a.ndim)
    return pl.pallas_call(
        scan_forward,
        grid=(steps,),
        in_specs=[
            row(inner, 0), row(inner, 1), row(3 * SUB, 2 * inner // (3 * SUB)), row(marks.shape[1]),
            whole(taps), whole(bias), whole(par), whole(skip), whole(gain),
        ],
        out_specs=[
            row(inner), row(inner), row(2 * SUB), row(chans), row(inner),
            pl.BlockSpec((1, SUB, inner), lambda i: (i, 0, 0)), row(SUB),
        ],
        out_shape=[
            jax.ShapeDtypeStruct((length, inner), BF),
            jax.ShapeDtypeStruct((length, inner), BF),
            jax.ShapeDtypeStruct((length, 2 * SUB), BF),
            jax.ShapeDtypeStruct((length, chans), BF),
            jax.ShapeDtypeStruct((length, inner), BF),
            jax.ShapeDtypeStruct((steps, SUB, inner), BF),
            jax.ShapeDtypeStruct((length, SUB), F32),
        ],
        scratch_shapes=[pltpu.VMEM((SUB, inner), F32), pltpu.VMEM((SUB + 8, chans), F32)],
        compiler_params=pltpu.CompilerParams(vmem_limit_bytes=40 << 20),
        cost_estimate=pl.CostEstimate(flops=2 << 30, bytes_accessed=14 << 20, transcendentals=6 << 20),
        name="scan_forward",
    )(gx, gx, gx, marks, taps, bias, par, skip, gain)


def run_backward(gx, xc, bc, slope, y, dn, states, scale, marks, taps, par, skip, gain, pick):
    length = gx.shape[0]
    inner = skip.shape[1]
    chans = taps.shape[1]
    steps = length // SUB
    row = lambda cols, at=0: pl.BlockSpec((SUB, cols), lambda i, at=at: (steps - 1 - i, at))
    whole = lambda a: pl.BlockSpec(a.shape, lambda i: (0,) * a.ndim)
    total = inner + chans + SUB
    return pl.pallas_call(
        scan_backward,
        grid=(steps,),
        in_specs=[
            row(inner), row(SUB, (inner + chans) // SUB), row(inner), row(2 * SUB), row(chans), row(inner), row(inner),
            pl.BlockSpec((1, SUB, inner), lambda i: (steps - 1 - i, 0, 0)),
            pl.BlockSpec((8, SUB), lambda i: (0, steps - 1 - i)),
            row(marks.shape[1]), whole(taps), whole(par), whole(skip), whole(gain), whole(pick),
        ],
        out_specs=row(total),
        out_shape=jax.ShapeDtypeStruct((length, total), BF),
        scratch_shapes=[
            pltpu.VMEM((SUB, inner), F32),
            pltpu.VMEM((SUB + 8, chans), F32),
            pltpu.VMEM((SUB, inner), F32),
            pltpu.VMEM((SUB, inner), F32),
            pltpu.VMEM((8, inner), F32),
        ],
        compiler_params=pltpu.CompilerParams(vmem_limit_bytes=40 << 20),
        cost_estimate=pl.CostEstimate(flops=4 << 30, bytes_accessed=16 << 20, transcendentals=6 << 20),
        name="scan_backward",
    )(gx, gx, xc, bc, slope, y, dn, states, scale, marks, taps, par, skip, gain, pick)


def shifted_by(value, axis, distance):
    size = lax.axis_size(axis)
    return lax.ppermute(value, axis, [(i, (i + distance) % size) for i in range(size)])


def spread(value, axis):
    size, me = lax.axis_size(axis), lax.axis_index(axis)
    out = jnp.zeros((size, *value.shape), value.dtype)
    out = lax.dynamic_update_index_in_dim(out, value, me, 0)
    for d in range(1, size):
        got = shifted_by(value, axis, d)
        out = lax.dynamic_update_index_in_dim(out, got, (me - d) % size, 0)
    return out


def collect(blocks, axis):
    size, me = lax.axis_size(axis), lax.axis_index(axis)
    total = lax.dynamic_index_in_dim(blocks, me, 0, False).astype(F32)
    for d in range(1, size):
        piece = lax.dynamic_index_in_dim(blocks, (me + d) % size, 0, False)
        total = total + shifted_by(piece, axis, d).astype(F32)
    return total


def summed(value, axis):
    total = value
    for d in range(1, lax.axis_size(axis)):
        total = total + shifted_by(value, axis, d)
    return total


def swapped(value, axis):
    return lax.all_to_all(value, axis, 0, 0, tiled=True)


def per_device(
    tokens, output_cotangent, segments, sequence_adapter, input_norm_gain,
    gate_x_projection_weight, bc_projection_weight, step_projection_weight,
    x_convolution_taps, x_convolution_bias, bc_convolution_taps, bc_convolution_bias,
    step_size_bias, log_decay_rate, head_skip_gain, gated_norm_gain, output_projection_weight,
    in_adapter_down, in_adapter_up, out_adapter_down, out_adapter_up,
):
    seqs, block, width = tokens.shape
    inner = gate_x_projection_weight.shape[2]
    heads = step_projection_weight.shape[1]
    rank = in_adapter_down.shape[2]
    ny, nz = lax.axis_size("tensor"), lax.axis_size("context")
    my, mz = lax.axis_index("tensor"), lax.axis_index("context")
    length = block * nz
    share = block // ny

    rows = gate_x_projection_weight.shape[0]
    packed = jnp.concatenate(
        [
            output_projection_weight.T,
            gate_x_projection_weight.reshape(rows, 2 * inner),
            bc_projection_weight,
            step_projection_weight,
            jnp.zeros((rows, SUB - heads), BF),
        ],
        1,
    )
    full = lax.all_gather(packed, ("fsdp", "context"), axis=0, tiled=True)
    w_out, w_in = full[:, :inner], full[:, inner:]

    seg = swapped(segments, "context").reshape(length)
    every_adapter = lax.all_gather(sequence_adapter, "fsdp", axis=0, tiled=True)
    mine = lax.dynamic_index_in_dim(sequence_adapter, mz, 0, False)
    down_in = lax.dynamic_index_in_dim(in_adapter_down.transpose(0, 2, 1), mine, 0, False)
    up_in = lax.dynamic_index_in_dim(in_adapter_up, mine, 0, False).reshape(rank, 2 * inner)
    down_out = lax.dynamic_index_in_dim(out_adapter_down.transpose(0, 2, 1), mine, 0, False)
    up_out = lax.dynamic_index_in_dim(out_adapter_up, mine, 0, False)

    tokens_q = lax.dynamic_slice_in_dim(tokens, my * share, share, 1).astype(F32)
    cot_q = lax.dynamic_slice_in_dim(output_cotangent, my * share, share, 1)
    rms = lax.rsqrt(jnp.mean(tokens_q * tokens_q, -1, keepdims=True) + EPS_NORM)
    normed_q = (tokens_q * rms * input_norm_gain).astype(BF)

    def own_sequence(quarter):
        return spread(swapped(quarter, "context"), "tensor").transpose(1, 0, 2, 3).reshape(length, width)

    normed = own_sequence(normed_q)
    cot = own_sequence(cot_q)

    pos = jnp.arange(length)
    by_sub = seg.reshape(-1, SUB)
    last = by_sub[:, -1]
    before = jnp.concatenate([jnp.full((1,), -1, seg.dtype), last[:-1]])
    back = [jnp.where(pos >= k, jnp.roll(seg, k) == seg, False) for k in (1, 2, 3)]
    forth = [jnp.where(pos < length - k, jnp.roll(seg, -k) == seg, False) for k in (1, 2, 3)]
    same = lambda v: jnp.broadcast_to(v[:, None], by_sub.shape)
    columns = [
        *back,
        (by_sub == same(before)).reshape(-1),
        (by_sub == same(last)).reshape(-1),
        seg,
        same(last == before).reshape(-1),
        *forth,
    ]
    marks = jnp.stack([c.astype(F32) for c in columns] + [jnp.zeros((length,), F32)] * 6, -1)

    taps = jnp.concatenate([x_convolution_taps, bc_convolution_taps], 1)
    conv_bias = jnp.concatenate([x_convolution_bias, bc_convolution_bias], 0)[None]
    par = jnp.zeros((8, SUB), F32)
    par = par.at[0, :heads].set(step_size_bias).at[1, :heads].set(-jnp.exp(log_decay_rate))
    skip = jnp.repeat(head_skip_gain, inner // heads)[None]
    gain = gated_norm_gain[None]
    pick = (jnp.arange(inner)[:, None] // (inner // heads) == jnp.arange(SUB)[None, :]).astype(BF)

    low_rank = dot_nt(normed, down_in).astype(BF)
    up_wide = jnp.pad(up_in, ((0, 0), (0, w_in.shape[1] - 2 * inner)))
    gx = (dot_nn(normed, w_in) + dot_nn(low_rank, up_wide)).astype(BF)
    y, xc, bc, slope, g2, states, square = run_forward(gx, marks, taps, conv_bias, par, skip, gain)
    d_low = dot_nt(cot, up_out).astype(BF)
    dn = (dot_nn(cot, w_out) + dot_nn(d_low, down_out)).astype(BF)
    norm_dot = jnp.sum(dn.astype(F32) * g2.astype(F32), -1)
    low_part = dot_nt(down_out, g2)
    stats = jnp.concatenate(
        [jnp.sum(square, -1)[None], norm_dot[None], jnp.zeros((6, length), F32), low_part], 0
    )
    stats = summed(stats, "tensor")
    rn = lax.rsqrt(stats[0:1] / INNER_CHANNELS + EPS_NORM)
    kappa = rn * rn * rn * stats[1:2] / INNER_CHANNELS
    scale = jnp.concatenate([rn, kappa, jnp.zeros((6, length), F32)], 0)
    low_out = (stats[8:] * rn).astype(BF)

    def by_owner(value):
        return value.reshape(nz, ny, share, width).transpose(1, 0, 2, 3)

    branch = collect(by_owner(dot_nt(g2, w_out).astype(BF)), "tensor").reshape(nz * share, width)
    my_rows = lambda v: lax.dynamic_index_in_dim(v.reshape(-1, nz, ny, share), my, 2, False).reshape(-1, nz * share)
    branch = branch * my_rows(rn)[0][:, None] + dot_tn(my_rows(low_out), up_out)
    branch = swapped(branch.astype(BF).reshape(nz, share, width), "context")
    out_q = (tokens_q + branch.astype(F32)).astype(BF)
    layer_out = spread(out_q, "tensor").transpose(1, 0, 2, 3).reshape(seqs, block, width)

    grad_out_b = dot_nn(low_out, cot)
    grad_out_a = dot_tn((d_low.astype(F32) * rn[0][:, None]).astype(BF), g2)

    d_all = run_backward(gx, xc, bc, slope, y, dn, states, scale, marks, taps, par, skip, gain, pick)
    d_gate = d_all[:, : 2 * inner]
    rank_part = dot_nt(d_gate, up_in).astype(BF)
    d_in = (dot_nt(d_all, w_in) + dot_nn(rank_part, down_in)).astype(BF)
    d_rank = summed(rank_part.astype(F32), "tensor").astype(BF)
    grad_in_b = dot_tn(low_rank, d_gate)
    grad_in_a = dot_tn(d_rank, normed)

    d_in_q = swapped(collect(by_owner(d_in), "tensor").astype(BF), "context").astype(F32)
    pulled = d_in_q * input_norm_gain
    grad_q = rms * pulled - tokens_q * (rms**3 * jnp.mean(pulled * tokens_q, -1, keepdims=True))
    grad_all = spread(grad_q.astype(BF), "tensor").transpose(1, 0, 2, 3).reshape(seqs, block, width)
    grad_tokens = grad_all.astype(F32) + output_cotangent.astype(F32)

    both = ("fsdp", "context")
    parts = lax.axis_size(both)
    mine_all = jnp.concatenate([grad_in_a, grad_in_b, grad_out_a, grad_out_b], 1).astype(BF)
    columns_all = mine_all.shape[1]
    slices = lax.all_to_all(mine_all.reshape(parts, -1), both, 0, 0, tiled=True)
    table = in_adapter_down.shape[0]
    chosen = (jnp.arange(table, dtype=jnp.int32)[:, None] == every_adapter[None, :]).astype(BF)
    mixed = dot_nn(chosen, slices).astype(BF)
    everything = lax.all_gather(mixed, both, axis=0)
    everything = everything.transpose(1, 0, 2).reshape(table, rank, columns_all).astype(F32)
    cut = jnp.split(everything, [width, width + 2 * inner, width + 3 * inner], 2)
    return (
        layer_out,
        grad_tokens,
        cut[0].transpose(0, 2, 1),
        cut[1].reshape(table, rank, 2, inner),
        cut[2].transpose(0, 2, 1),
        cut[3],
    )


def solution(mesh):
    placed = (
        P("fsdp", "context", None),
        P("fsdp", "context", None),
        P("fsdp", "context"),
        P("fsdp"),
        P(),
        P(("fsdp", "context"), None, "tensor"),
        P(("fsdp", "context"), None),
        P(("fsdp", "context"), "tensor"),
        P(None, "tensor"),
        P("tensor"),
        P(),
        P(),
        P("tensor"),
        P("tensor"),
        P("tensor"),
        P("tensor"),
        P("tensor", ("fsdp", "context")),
        P(),
        P(None, None, None, "tensor"),
        P(None, "tensor", None),
        P(),
    )
    return jax.shard_map(
        per_device,
        mesh=mesh,
        in_specs=placed,
        out_specs=(
            P("fsdp", "context", None),
            P("fsdp", "context", None),
            P(),
            P(None, None, None, "tensor"),
            P(None, "tensor", None),
            P(),
        ),
        check_vma=False,
    )
```

time: 678 us -> 391 us (0.58)
  matrix products: 157 us -> 51.6 us
  waiting for transfers between devices: 236 us -> 139 us
  other arithmetic: 98.4 us -> 25.7 us
  local copies, waits for them, and re-layouts: 101 us -> 40.4 us
  starting transfers between devices: 36.8 us -> 70 us
  Pallas kernels: 0 us -> 32.6 us
  blocking collectives: 21.2 us -> 8.11 us
    ppermute x3 -> x24, waiting for transfers between devices: 3.94 us -> 111 us  [shifted_by(): lax.ppermute(value, axis, [(i, (i + distance) % size) for i in range(size)])]
    dot_general x41 -> x17, matrix products: 157 us -> 51.6 us  [the longest x7 28 us: dot_nn(): lax.dot_general(a, b, (((1,), (0,)), ((), ())), preferred_element_type=F32)]
    psum x2 -> x0, waiting for transfers between devices: 90.5 us -> none  [the longest x1 61.4 us: per_device(): lax.psum(head_part.astype(jnp.bfloat16), 'tensor').astype(jnp.float32)]
    all_gather x4 -> x2, waiting for transfers between devices: 88.1 us -> 0.01 us  [the longest x1 0.01 us: per_device(): full = lax.all_gather(packed, ('fsdp', 'context'), axis=0, tiled=True)]
    pallas_call x0 -> x2, Pallas kernels: none -> 32.6 us  [the longest x1 20.9 us: run_backward(): pl.pallas_call(scan_backward, grid=(steps,), in_specs=[row(inner), row(SU...]
    ppermute x3 -> x24, starting transfers between devices: 8.81 us -> 40.2 us  [shifted_by(): lax.ppermute(value, axis, [(i, (i + distance) % size) for i in range(size)])]
    all_to_all x6, waiting for transfers between devices: 52.6 us -> 28.8 us  [the longest x5 26.7 us: swapped(): return lax.all_to_all(value, axis, 0, 0, tiled=True)]
    another operation x8 -> x1, other arithmetic: 23.9 us -> 0.66 us
  transfers between devices with their start and end apart: 15 -> 32, of which waited for: 9 -> 12; matrix products, arithmetic and copies ran while one was open for 27% -> 19% of each run, Pallas kernels for 0% -> 5%
where the time goes in v1:
time: 391 us; the launch traced here: 386 us
  waiting for transfers between devices  139 us (36%)
  starting transfers between devices  70 us (18%)
  matrix products  51.6 us (13%)
  local copies, waits for them, and re-layouts  40.4 us (10%)
  Pallas kernels  32.6 us (8%)
  other arithmetic  25.7 us (7%)
  between operations  17.9 us (5%)
  blocking collectives  8.11 us (2%)
    ppermute x24, waiting for transfers between devices, shifted_by(): lax.ppermute(value, axis, [(i, (i + distance) % size) for i in range(size)])  111 us
    ppermute x24, starting transfers between devices, shifted_by(): lax.ppermute(value, axis, [(i, (i + distance) % size) for i in range(size)])  40.2 us
    dot_general x7, matrix products, dot_nn(): lax.dot_general(a, b, (((1,), (0,)), ((), ())), preferred_element_type=F32)  28 us
    all_to_all x5, waiting for transfers between devices, swapped(): return lax.all_to_all(value, axis, 0, 0, tiled=True)  26.7 us
    all_to_all x5, starting transfers between devices, swapped(): return lax.all_to_all(value, axis, 0, 0, tiled=True)  22.4 us
    pallas_call x1, Pallas kernels, run_backward(): pl.pallas_call(scan_backward, grid=(steps,), in_specs=[row(inner), row(SU...  20.9 us
    dot_general x6, matrix products, dot_nt(): lax.dot_general(a, b, (((1,), (1,)), ((), ())), preferred_element_type=F32)  18.2 us
    unnamed x77, local copies, waits for them, and re-layouts  13.4 us
  transfers between devices with their start and end apart: 32, of which 12 were waited for; matrix products, arithmetic and copies ran while one was open for 19% of the time, Pallas kernels for 5%

profile of v1, /device:TPU:0, one launch (start us, length us, event | category | flops | bytes accessed | tf_op | source)
XLA Modules:
  0.0 385.7 jit_solution(12088599871076815366)
XLA Ops:
  12.0 5.4 %all-to-all-start.1 = ((s32[4,1,256]{2,1,0:T(1,128)}), s32[4,1,256]{2,1,0:T(1,128)S(1)}, u32[]{:S(2)}, u32[]{:S(2)}) async-start(s32[4,1,256]{2,1,0:T(1,128)} %all_to_all.25), calls=%async_computation.1 | async-start | bytes 8192 | tf_op jit(solution)/shard_map/all_to_all | solution.py:328
  30.6 4.8 %all-to-all-start = ((bf16[4,64,1536]{2,1,0:T(8,128)(2,1)}), bf16[4,64,1536]{2,1,0:T(8,128)(2,1)S(1)}, u32[]{:S(2)}, u32[]{:S(2)}) async-start(bf16[4,64,1536]{2,1,0:T(8,128)(2,1)} %fusion.18), calls=%async_computation | async-start | bytes 1572864 | tf_op jit(solution)/shard_map/all_to_all | solution.py:328
  36.2 11.0 %all-to-all-done = bf16[4,64,1536]{2,1,0:T(8,128)(2,1)S(1)} async-done(((bf16[4,64,1536]{2,1,0:T(8,128)(2,1)}), bf16[4,64,1536]{2,1,0:T(8,128)(2,1)S(1)}, u32[]{:S(2)}, u32[]{:S(2)}) %all-to-all-start) | async-done | bytes 786464 | tf_op jit(solution)/shard_map/all_to_all | solution.py:328
  47.1 3.5 all-to-all-start.2
  54.9 2.9 collective-permute-start.1
  57.8 13.9 %all-to-all-done.2 = bf16[4,64,1536]{2,1,0:T(8,128)(2,1)S(1)} async-done(((bf16[4,64,1536]{2,1,0:T(8,128)(2,1)}), bf16[4,64,1536]{2,1,0:T(8,128)(2,1)S(1)}, u32[]{:S(2)}, u32[]{:S(2)}) %all-to-all-start.2) | async-done | bytes 786464 | tf_op jit(solution)/shard_map/all_to_all | solution.py:328
  73.3 2.9 collective-permute-start.7
  79.8 27.8 %collective-permute-done.6 = bf16[4,64,1536]{2,1,0:T(8,128)(2,1)S(1)} collective-permute-done((bf16[4,64,1536]{2,1,0:T(8,128)(2,1)S(1)}, bf16[4,64,1536]{2,1,0:T(8,128)(2,1)S(1)}, u32[]{:S(2)}, u32[]{:S(2)}) %collective-permute-start.6) | collective-permute-done | bytes 786464 | tf_op jit(solution)/shard_map/ppermute | solution.py:298
  107.7 16.2 %collective-permute-done.7 = bf16[4,64,1536]{2,1,0:T(8,128)(2,1)S(1)} collective-permute-done((bf16[4,64,1536]{2,1,0:T(8,128)(2,1)S(1)}, bf16[4,64,1536]{2,1,0:T(8,128)(2,1)S(1)}, u32[]{:S(2)}, u32[]{:S(2)}) %collective-permute-start.7) | collective-permute-done | bytes 786464 | tf_op jit(solution)/shard_map/ppermute | solution.py:298
  126.9 3.0 fusion.55
  129.9 4.3 %fusion.39 = f32[1024,1920]{1,0:T(8,128)} fusion(bf16[1024,16]{0,1:T(8,128)(2,1)S(1)} %convolution_convert_fusion.5, bf16[16,1536]{1,0:T(8,128)(2,1)S(1)} %bitcast.221), kind=kOutput, calls=%fused_computation.84 | convolution fusion | flops 62914560 | bytes 7946240 | tf_op jit(solution)/shard_map/dot_general | solution.py:20
  134.2 11.2 %add_convert_fusion.z_ref.x_ref.bcdt_ref.dt_ref = bf16[1024,1920]{1,0:T(8,128)(2,1)S(1)} fusion(f32[1024,1920]{1,0:T(8,128)} %fusion.39, bf16[1024,1536]{1,0:T(8,128)(2,1)} %bitcast.202, bf16[1536,2688]{1,0:T(8,128)(2,1)} %all-gather.4.cloned.1.call-done), kind=kOutput, calls=%fused_computation | convolution fusion | flops 6043729920 | bytes 20840448 | tf_op jit(solution)/shard_map/dot_general | solution.py:20
  145.4 11.7 %scan_forward.1 = (bf16[1024,768]{1,0:T(8,128)(2,1)S(1)}, bf16[1024,768]{1,0:T(8,128)(2,1)S(1)}, bf16[1024,256]{1,0:T(8,128)(2,1)S(1)}, bf16[1024,1024]{1,0:T(8,...) custom-call(bf16[1024,1920]{1,0:T(8,128)(2,1)S(1)} %add_convert_fusion.z_ref, ...), custom_call_target="tpu_custom_call" | custom-call | flops 2147483648 | bytes 14680064 | tf_op jit(solution)/shard_map/scan_forward/pallas_call | solution.py:237
  165.3 6.3 %multiply_reduce_fusion = (f32[1024]{0:T(1024)S(1)}, bf16[1024,768]{1,0:T(8,128)(2,1)S(1)}) fusion(bf16[1024,768]{1,0:T(8,128)(2,1)S(1)} %get-tuple-element.37, f32[1024,768]{1,0:T(8,128)} %fusion.55, bf16[1024,1536]{1,0:T(8,128)(2,1)} %bitcast.199, bf16[1536,2688]{1,0:T(8,128)(2,1)} %all-gather.4.cloned.1.call-done), kind=kOutput, calls=%fused_computation.9 | convolution fusion | flops 2420636672 | bytes 11800576 | tf_op jit(solution)/shard_map/dot_general | solution.py:20
  171.6 3.2 collective-permute-start.10
  176.8 4.6 %convolution_convert_fusion = bf16[1024,1536]{1,0:T(8,128)(2,1)S(1)} fusion(bf16[1024,768]{1,0:T(8,128)(2,1)S(1)} %get-tuple-element.37, bf16[1536,2688]{1,0:T(8,128)(2,1)} %all-gather.4.cloned.1.call-done), kind=kOutput, calls=%fused_computation.7 | convolution fusion | flops 2417491968 | bytes 7077888 | tf_op jit(solution)/shard_map/dot_general | solution.py:24
  183.3 3.9 %collective-permute-start.4 = (bf16[4,64,1536]{2,1,0:T(8,128)(2,1)}, bf16[4,64,1536]{2,1,0:T(8,128)(2,1)}, u32[]{:S(2)}, u32[]{:S(2)}) collective-permute-start(bf16[4,64,1536]{2,1,0:T(8,128)(2,1)} %get-tuple-element.55), channel_id=1, source_target_pairs={{0,2},{1,3},{2,0},{3,1},{4,6},{5,7},{6,4},{7,5},{8,10},{9,11},{10,... | collective-permute-start | bytes 2359304 | tf_op jit(solution)/shard_map/ppermute | solution.py:298
  187.3 20.9 %scan_backward.1 = bf16[1024,1920]{1,0:T(8,128)(2,1)S(1)} custom-call(bf16[1024,1920]{1,0:T(8,128)(2,1)} %copy-done.1, bf16[1024,1920]{1,0:T(8,128)(2,1)} %copy-done.1, bf16[1024,768]{1,0:T(8,128)(2,1)S(1)} %copy-done.7, bf16[1024,256]{1,0:T(8,128)(2,1)S(1)} %get-tuple-element.40.bc_ref, bf16[1024,1024]{1,0:T(8,128)(2,1)S(1)} %copy-done.3, ...), custom_call_target="tpu_custom_call" | custom-call | flops 4294967296 | bytes 16777216 | tf_op jit(solution)/shard_map/scan_backward/pallas_call | solution.py:272
  213.5 8.8 %fusion = f32[1024,1536]{1,0:T(8,128)S(1)} fusion(bf16[1024,1920]{1,0:T(8,128)(2,1)S(1)} %scan_backward.1, bf16[1536,2688]{1,0:T(8,128)(2,1)} %all-gather.4.cloned.1.call-done), kind=kOutput, calls=%fused_computation.3 | convolution fusion | flops 6039797760 | bytes 16121856 | tf_op jit(solution)/shard_map/dot_general | solution.py:24
  231.1 2.9 collective-permute-start.16
  239.6 7.3 %all-to-all-start.5 = ((bf16[32,2,1344]{2,1,0:T(2,128)(2,1)}), bf16[32,2,1344]{2,1,0:T(2,128)(2,1)S(1)}, u32[]{:S(2)}, u32[]{:S(2)}) async-start(bf16[32,2,1344]{2,1,0:T(2,128)(2,1)} %reshape.647), calls=%async_computation.5 | async-start | bytes 360448 | tf_op jit(solution)/shard_map/all_to_all | solution.py:453
  255.3 3.5 all-to-all-start.3
  260.3 8.1 %all-reduce.2 = s32[32]{0:T(128)S(1)} all-reduce(s32[32]{0:T(128)S(1)} %dynamic-update-slice.4), channel_id=1, replica_groups=mesh['fsdp'=8,'context'=4,'tensor'=4] {'fsdp'}, use_global_device_ids=true, to_apply=%add.2 | all-reduce | flops 32 | bytes 256
  269.4 9.9 %collective-permute-done.17 = bf16[4,64,1536]{2,1,0:T(8,128)(2,1)} collective-permute-done((bf16[4,64,1536]{2,1,0:T(8,128)(2,1)}, bf16[4,64,1536]{2,1,0:T(8,128)(2,1)}, u32[]{:S(2)}, u32[]{:S(2)}) %collective-permute-start.17) | collective-permute-done | bytes 786464 | tf_op jit(solution)/shard_map/ppermute | solution.py:298
  279.3 2.6 fusion.25
  281.9 5.2 %all-to-all-start.4 = ((bf16[4,64,1536]{2,1,0:T(8,128)(2,1)}), bf16[4,64,1536]{2,1,0:T(8,128)(2,1)S(1)}, u32[]{:S(2)}, u32[]{:S(2)}) async-start(bf16[4,64,1536]{2,1,0:T(8,128)(2,1)} %fusion.25), calls=%async_computation.4 | async-start | bytes 1572864 | tf_op jit(solution)/shard_map/all_to_all | solution.py:328
  302.0 2.6 collective-permute-start.18
  307.3 22.1 %collective-permute-done.12 = bf16[4,64,1536]{2,1,0:T(8,128)(2,1)S(1)} collective-permute-done((bf16[4,64,1536]{2,1,0:T(8,128)(2,1)}, bf16[4,64,1536]{2,1,0:T(8,128)(2,1)S(1)}, u32[]{:S(2)}, u32[]{:S(2)}) %collective-permute-start.12) | collective-permute-done | bytes 786464 | tf_op jit(solution)/shard_map/ppermute | solution.py:298
  331.2 14.2 %collective-permute-done.18 = bf16[4,64,1536]{2,1,0:T(8,128)(2,1)S(1)} collective-permute-done((bf16[4,64,1536]{2,1,0:T(8,128)(2,1)S(1)}, bf16[4,64,1536]{2,1,0:T(8,128)(2,1)S(1)}, u32[]{:S(2)}, u32[]{:S(2)}) %collective-permute-start.18) | collective-permute-done | bytes 786464 | tf_op jit(solution)/shard_map/ppermute | solution.py:298
  345.5 18.0 %collective-permute-done.19 = bf16[4,64,1536]{2,1,0:T(8,128)(2,1)S(1)} collective-permute-done((bf16[4,64,1536]{2,1,0:T(8,128)(2,1)S(1)}, bf16[4,64,1536]{2,1,0:T(8,128)(2,1)S(1)}, u32[]{:S(2)}, u32[]{:S(2)}) %collective-permute-start.19) | collective-permute-done | bytes 786464 | tf_op jit(solution)/shard_map/ppermute | solution.py:298
  363.7 3.7 bitcast_add_fusion
  370.9 2.7 reshape.623
  (221 shorter events, 98.7 us)
Async XLA Ops:
  7.2 127.0 %all-gather.4.cloned.1.call-start = ((), (), s32[]{:S(2)}) async-start(), calls=%async_computation.6 | async-start | bytes 8515584 | tf_op jit(solution)/shard_map/all_gather | solution.py:358
  12.0 18.6 %all-to-all-start.1 = ((s32[4,1,256]{2,1,0:T(1,128)}), s32[4,1,256]{2,1,0:T(1,128)S(1)}, u32[]{:S(2)}, u32[]{:S(2)}) async-start(s32[4,1,256]{2,1,0:T(1,128)} %all_to_all.25), calls=%async_computation.1 | async-start | bytes 8192 | tf_op jit(solution)/shard_map/all_to_all | solution.py:328
  30.6 16.6 %all-to-all-start = ((bf16[4,64,1536]{2,1,0:T(8,128)(2,1)}), bf16[4,64,1536]{2,1,0:T(8,128)(2,1)S(1)}, u32[]{:S(2)}, u32[]{:S(2)}) async-start(bf16[4,64,1536]{2,1,0:T(8,128)(2,1)} %fusion.18), calls=%async_computation | async-start | bytes 1572864 | tf_op jit(solution)/shard_map/all_to_all | solution.py:328
  47.1 24.6 %all-to-all-start.2 = ((bf16[4,64,1536]{2,1,0:T(8,128)(2,1)}), bf16[4,64,1536]{2,1,0:T(8,128)(2,1)S(1)}, u32[]{:S(2)}, u32[]{:S(2)}) async-start(bf16[4,64,1536]{2,1,0:T(8,128)(2,1)} %constant_dynamic-slice_fusion.1), calls=%async_computation.2 | async-start | bytes 1572864 | tf_op jit(solution)/shard_map/all_to_all | solution.py:328
  53.3 25.0 %collective-permute-start = (bf16[4,64,1536]{2,1,0:T(8,128)(2,1)S(1)}, bf16[4,64,1536]{2,1,0:T(8,128)(2,1)}, u32[]{:S(2)}, u32[]{:S(2)}) collective-permute-start(bf16[4,64,1536]{2,1,0:T(8,128)(2,1)S(1)} %all-to-all-done), channel_id=1, source_target_pairs={{0,1},{1,2},{2,3},{3,0},{4,5},{5,6},{6,7},{7,4},{8,9},{9,10},{10,1... | collective-permute-start | bytes 2359304 | tf_op jit(solution)/shard_map/ppermute | solution.py:298
  54.9 52.7 %collective-permute-start.1 = (bf16[4,64,1536]{2,1,0:T(8,128)(2,1)S(1)}, bf16[4,64,1536]{2,1,0:T(8,128)(2,1)S(1)}, u32[]{:S(2)}, u32[]{:S(2)}) collective-permute-start(bf16[4,64,1536]{2,1,0:T(8,128)(2,1)S(1)} %all-to-all-done), channel_id=1, source_target_pairs={{0,2},{1,3},{2,0},{3,1},{4,6},{5,7},{6,4},{7,5},{8,10},{9,11},{10,... | collective-permute-start | bytes 2359304 | tf_op jit(solution)/shard_map/ppermute | solution.py:298
  71.7 35.9 %collective-permute-start.6 = (bf16[4,64,1536]{2,1,0:T(8,128)(2,1)S(1)}, bf16[4,64,1536]{2,1,0:T(8,128)(2,1)S(1)}, u32[]{:S(2)}, u32[]{:S(2)}) collective-permute-start(bf16[4,64,1536]{2,1,0:T(8,128)(2,1)S(1)} %all-to-all-done.2), channel_id=1, source_target_pairs={{0,1},{1,2},{2,3},{3,0},{4,5},{5,6},{6,7},{7,4},{8,9},{9,10},{10,1... | collective-permute-start | bytes 2359304 | tf_op jit(solution)/shard_map/ppermute | solution.py:298
  73.3 50.6 %collective-permute-start.7 = (bf16[4,64,1536]{2,1,0:T(8,128)(2,1)S(1)}, bf16[4,64,1536]{2,1,0:T(8,128)(2,1)S(1)}, u32[]{:S(2)}, u32[]{:S(2)}) collective-permute-start(bf16[4,64,1536]{2,1,0:T(8,128)(2,1)S(1)} %all-to-all-done.2), channel_id=1, source_target_pairs={{0,2},{1,3},{2,0},{3,1},{4,6},{5,7},{6,4},{7,5},{8,10},{9,11},{10,... | collective-permute-start | bytes 2359304 | tf_op jit(solution)/shard_map/ppermute | solution.py:298
  76.2 47.8 %collective-permute-start.2 = (bf16[4,64,1536]{2,1,0:T(8,128)(2,1)S(1)}, bf16[4,64,1536]{2,1,0:T(8,128)(2,1)S(1)}, u32[]{:S(2)}, u32[]{:S(2)}) collective-permute-start(bf16[4,64,1536]{2,1,0:T(8,128)(2,1)S(1)} %all-to-all-done), channel_id=1, source_target_pairs={{0,3},{1,0},{2,1},{3,2},{4,7},{5,4},{6,5},{7,6},{8,11},{9,8},{10,9... | collective-permute-start | bytes 2359304 | tf_op jit(solution)/shard_map/ppermute | solution.py:298
  78.3 45.7 %collective-permute-start.8 = (bf16[4,64,1536]{2,1,0:T(8,128)(2,1)S(1)}, bf16[4,64,1536]{2,1,0:T(8,128)(2,1)S(1)}, u32[]{:S(2)}, u32[]{:S(2)}) collective-permute-start(bf16[4,64,1536]{2,1,0:T(8,128)(2,1)S(1)} %all-to-all-done.2), channel_id=1, source_target_pairs={{0,3},{1,0},{2,1},{3,2},{4,7},{5,4},{6,5},{7,6},{8,11},{9,8},{10,9... | collective-permute-start | bytes 2359304 | tf_op jit(solution)/shard_map/ppermute | solution.py:298
  171.6 15.6 %collective-permute-start.10 = (f32[24,1024]{1,0:T(8,128)S(1)}, f32[24,1024]{1,0:T(8,128)S(1)}, u32[]{:S(2)}, u32[]{:S(2)}) collective-permute-start(f32[24,1024]{1,0:T(8,128)S(1)} %pad_maximum_fusion.1), channel_id=1, source_target_pairs={{0,2},{1,3},{2,0},{3,1},{4,6},{5,7},{6,4},{7,5},{8,10},{9,11},{10,... | collective-permute-start | bytes 294920 | tf_op jit(solution)/shard_map/ppermute | solution.py:298
  174.8 12.4 %collective-permute-start.11 = (f32[24,1024]{1,0:T(8,128)S(1)}, f32[24,1024]{1,0:T(8,128)S(1)}, u32[]{:S(2)}, u32[]{:S(2)}) collective-permute-start(f32[24,1024]{1,0:T(8,128)S(1)} %pad_maximum_fusion.1), channel_id=1, source_target_pairs={{0,3},{1,0},{2,1},{3,2},{4,7},{5,4},{6,5},{7,6},{8,11},{9,8},{10,9... | collective-permute-start | bytes 294920 | tf_op jit(solution)/shard_map/ppermute | solution.py:298
  176.1 11.1 %collective-permute-start.9 = (f32[24,1024]{1,0:T(8,128)S(1)}, f32[24,1024]{1,0:T(8,128)S(1)}, u32[]{:S(2)}, u32[]{:S(2)}) collective-permute-start(f32[24,1024]{1,0:T(8,128)S(1)} %pad_maximum_fusion.1), channel_id=1, source_target_pairs={{0,1},{1,2},{2,3},{3,0},{4,5},{5,6},{6,7},{7,4},{8,9},{9,10},{10,1... | collective-permute-start | bytes 294920 | tf_op jit(solution)/shard_map/ppermute | solution.py:298
  183.0 64.0 %collective-permute-start.3 = (bf16[4,64,1536]{2,1,0:T(8,128)(2,1)}, bf16[4,64,1536]{2,1,0:T(8,128)(2,1)}, u32[]{:S(2)}, u32[]{:S(2)}) collective-permute-start(bf16[4,64,1536]{2,1,0:T(8,128)(2,1)} %get-tuple-element.53), channel_id=1, source_target_pairs={{0,1},{1,2},{2,3},{3,0},{4,5},{5,6},{6,7},{7,4},{8,9},{9,10},{10,1... | collective-permute-start | bytes 2359304 | tf_op jit(solution)/shard_map/ppermute | solution.py:298
  183.3 65.1 %collective-permute-start.4 = (bf16[4,64,1536]{2,1,0:T(8,128)(2,1)}, bf16[4,64,1536]{2,1,0:T(8,128)(2,1)}, u32[]{:S(2)}, u32[]{:S(2)}) collective-permute-start(bf16[4,64,1536]{2,1,0:T(8,128)(2,1)} %get-tuple-element.55), channel_id=1, source_target_pairs={{0,2},{1,3},{2,0},{3,1},{4,6},{5,7},{6,4},{7,5},{8,10},{9,11},{10,... | collective-permute-start | bytes 2359304 | tf_op jit(solution)/shard_map/ppermute | solution.py:298
  209.2 19.2 %collective-permute-start.21 = (f32[1024,16]{0,1:T(8,128)S(1)}, f32[1024,16]{0,1:T(8,128)S(1)}, u32[]{:S(2)}, u32[]{:S(2)}) collective-permute-start(f32[1024,16]{0,1:T(8,128)S(1)} %get-tuple-element.81), channel_id=1, source_target_pairs={{0,1},{1,2},{2,3},{3,0},{4,5},{5,6},{6,7},{7,4},{8,9},{9,10},{10,1... | collective-permute-start | bytes 196616 | tf_op jit(solution)/shard_map/ppermute | solution.py:298
  209.3 20.1 %collective-permute-start.22 = (f32[1024,16]{0,1:T(8,128)S(1)}, f32[1024,16]{0,1:T(8,128)S(1)}, u32[]{:S(2)}, u32[]{:S(2)}) collective-permute-start(f32[1024,16]{0,1:T(8,128)S(1)} %get-tuple-element.81), channel_id=1, source_target_pairs={{0,2},{1,3},{2,0},{3,1},{4,6},{5,7},{6,4},{7,5},{8,10},{9,11},{10,... | collective-permute-start | bytes 196616 | tf_op jit(solution)/shard_map/ppermute | solution.py:298
  211.8 18.6 %collective-permute-start.23 = (f32[1024,16]{0,1:T(8,128)S(1)}, f32[1024,16]{0,1:T(8,128)S(1)}, u32[]{:S(2)}, u32[]{:S(2)}) collective-permute-start(f32[1024,16]{0,1:T(8,128)S(1)} %get-tuple-element.81), channel_id=1, source_target_pairs={{0,3},{1,0},{2,1},{3,2},{4,7},{5,4},{6,5},{7,6},{8,11},{9,8},{10,9... | collective-permute-start | bytes 196616 | tf_op jit(solution)/shard_map/ppermute | solution.py:298
  228.4 20.7 %collective-permute-start.5 = (bf16[4,64,1536]{2,1,0:T(8,128)(2,1)}, bf16[4,64,1536]{2,1,0:T(8,128)(2,1)S(1)}, u32[]{:S(2)}, u32[]{:S(2)}) collective-permute-start(bf16[4,64,1536]{2,1,0:T(8,128)(2,1)} %get-tuple-element.54), channel_id=1, source_target_pairs={{0,3},{1,0},{2,1},{3,2},{4,7},{5,4},{6,5},{7,6},{8,11},{9,8},{10,9... | collective-permute-start | bytes 2359304 | tf_op jit(solution)/shard_map/ppermute | solution.py:298
  229.3 40.0 %collective-permute-start.15 = (bf16[4,64,1536]{2,1,0:T(8,128)(2,1)}, bf16[4,64,1536]{2,1,0:T(8,128)(2,1)S(1)}, u32[]{:S(2)}, u32[]{:S(2)}) collective-permute-start(bf16[4,64,1536]{2,1,0:T(8,128)(2,1)} %get-tuple-element.50), channel_id=1, source_target_pairs={{0,1},{1,2},{2,3},{3,0},{4,5},{5,6},{6,7},{7,4},{8,9},{9,10},{10,1... | collective-permute-start | bytes 2359304 | tf_op jit(solution)/shard_map/ppermute | solution.py:298
  231.1 38.3 %collective-permute-start.16 = (bf16[4,64,1536]{2,1,0:T(8,128)(2,1)}, bf16[4,64,1536]{2,1,0:T(8,128)(2,1)S(1)}, u32[]{:S(2)}, u32[]{:S(2)}) collective-permute-start(bf16[4,64,1536]{2,1,0:T(8,128)(2,1)} %get-tuple-element.52), channel_id=1, source_target_pairs={{0,2},{1,3},{2,0},{3,1},{4,6},{5,7},{6,4},{7,5},{8,10},{9,11},{10,... | collective-permute-start | bytes 2359304 | tf_op jit(solution)/shard_map/ppermute | solution.py:298
  239.6 15.7 %all-to-all-start.5 = ((bf16[32,2,1344]{2,1,0:T(2,128)(2,1)}), bf16[32,2,1344]{2,1,0:T(2,128)(2,1)S(1)}, u32[]{:S(2)}, u32[]{:S(2)}) async-start(bf16[32,2,1344]{2,1,0:T(2,128)(2,1)} %reshape.647), calls=%async_computation.5 | async-start | bytes 360448 | tf_op jit(solution)/shard_map/all_to_all | solution.py:453
  247.0 32.3 %collective-permute-start.17 = (bf16[4,64,1536]{2,1,0:T(8,128)(2,1)}, bf16[4,64,1536]{2,1,0:T(8,128)(2,1)}, u32[]{:S(2)}, u32[]{:S(2)}) collective-permute-start(bf16[4,64,1536]{2,1,0:T(8,128)(2,1)} %get-tuple-element.51), channel_id=1, source_target_pairs={{0,3},{1,0},{2,1},{3,2},{4,7},{5,4},{6,5},{7,6},{8,11},{9,8},{10,9... | collective-permute-start | bytes 2359304 | tf_op jit(solution)/shard_map/ppermute | solution.py:298
  255.3 26.6 %all-to-all-start.3 = ((bf16[4,64,1536]{2,1,0:T(8,128)(2,1)}), bf16[4,64,1536]{2,1,0:T(8,128)(2,1)S(1)}, u32[]{:S(2)}, u32[]{:S(2)}) async-start(bf16[4,64,1536]{2,1,0:T(8,128)(2,1)} %bitcast.63), calls=%async_computation.3 | async-start | bytes 1572864 | tf_op jit(solution)/shard_map/all_to_all | solution.py:328
  281.9 16.6 %all-to-all-start.4 = ((bf16[4,64,1536]{2,1,0:T(8,128)(2,1)}), bf16[4,64,1536]{2,1,0:T(8,128)(2,1)S(1)}, u32[]{:S(2)}, u32[]{:S(2)}) async-start(bf16[4,64,1536]{2,1,0:T(8,128)(2,1)} %fusion.25), calls=%async_computation.4 | async-start | bytes 1572864 | tf_op jit(solution)/shard_map/all_to_all | solution.py:328
  287.1 80.3 %all-gather.6.cloned.1.call-start = ((), (), s32[]{:S(2)}) async-start(), calls=%async_computation.7 | async-start | bytes 1419264 | tf_op jit(solution)/shard_map/all_gather | solution.py:457
  291.5 37.9 %collective-permute-start.12 = (bf16[4,64,1536]{2,1,0:T(8,128)(2,1)}, bf16[4,64,1536]{2,1,0:T(8,128)(2,1)S(1)}, u32[]{:S(2)}, u32[]{:S(2)}) collective-permute-start(bf16[4,64,1536]{2,1,0:T(8,128)(2,1)} %get-tuple-element.49), channel_id=1, source_target_pairs={{0,1},{1,2},{2,3},{3,0},{4,5},{5,6},{6,7},{7,4},{8,9},{9,10},{10,1... | collective-permute-start | bytes 2359304 | tf_op jit(solution)/shard_map/ppermute | solution.py:298
  293.1 38.0 %collective-permute-start.13 = (bf16[4,64,1536]{2,1,0:T(8,128)(2,1)}, bf16[4,64,1536]{2,1,0:T(8,128)(2,1)S(1)}, u32[]{:S(2)}, u32[]{:S(2)}) collective-permute-start(bf16[4,64,1536]{2,1,0:T(8,128)(2,1)} %get-tuple-element.49), channel_id=1, source_target_pairs={{0,2},{1,3},{2,0},{3,1},{4,6},{5,7},{6,4},{7,5},{8,10},{9,11},{10,... | collective-permute-start | bytes 2359304 | tf_op jit(solution)/shard_map/ppermute | solution.py:298
  295.5 35.6 %collective-permute-start.14 = (bf16[4,64,1536]{2,1,0:T(8,128)(2,1)}, bf16[4,64,1536]{2,1,0:T(8,128)(2,1)S(1)}, u32[]{:S(2)}, u32[]{:S(2)}) collective-permute-start(bf16[4,64,1536]{2,1,0:T(8,128)(2,1)} %get-tuple-element.49), channel_id=1, source_target_pairs={{0,3},{1,0},{2,1},{3,2},{4,7},{5,4},{6,5},{7,6},{8,11},{9,8},{10,9... | collective-permute-start | bytes 2359304 | tf_op jit(solution)/shard_map/ppermute | solution.py:298
  302.0 43.4 %collective-permute-start.18 = (bf16[4,64,1536]{2,1,0:T(8,128)(2,1)S(1)}, bf16[4,64,1536]{2,1,0:T(8,128)(2,1)S(1)}, u32[]{:S(2)}, u32[]{:S(2)}) collective-permute-start(bf16[4,64,1536]{2,1,0:T(8,128)(2,1)S(1)} %get-tuple-element.45), channel_id=1, source_target_pairs={{0,1},{1,2},{2,3},{3,0},{4,5},{5,6},{6,7},{7,4},{8,9},{9,10},{10,1... | collective-permute-start | bytes 2359304 | tf_op jit(solution)/shard_map/ppermute | solution.py:298
  304.7 58.9 %collective-permute-start.19 = (bf16[4,64,1536]{2,1,0:T(8,128)(2,1)S(1)}, bf16[4,64,1536]{2,1,0:T(8,128)(2,1)S(1)}, u32[]{:S(2)}, u32[]{:S(2)}) collective-permute-start(bf16[4,64,1536]{2,1,0:T(8,128)(2,1)S(1)} %get-tuple-element.45), channel_id=1, source_target_pairs={{0,2},{1,3},{2,0},{3,1},{4,6},{5,7},{6,4},{7,5},{8,10},{9,11},{10,... | collective-permute-start | bytes 2359304 | tf_op jit(solution)/shard_map/ppermute | solution.py:298
  329.3 34.3 %collective-permute-start.20 = (bf16[4,64,1536]{2,1,0:T(8,128)(2,1)S(1)}, bf16[4,64,1536]{2,1,0:T(8,128)(2,1)S(1)}, u32[]{:S(2)}, u32[]{:S(2)}) collective-permute-start(bf16[4,64,1536]{2,1,0:T(8,128)(2,1)S(1)} %get-tuple-element.45), channel_id=1, source_target_pairs={{0,3},{1,0},{2,1},{3,2},{4,7},{5,4},{6,5},{7,6},{8,11},{9,8},{10,9... | collective-permute-start | bytes 2359304 | tf_op jit(solution)/shard_map/ppermute | solution.py:298
  (33 other events, 426.4 us)
Sparse Core Ops, SparseCore 0:
  11.0 63.5 all-gather.3
  290.8 44.5 all-gather.5

commit v2 on v1

v2 whole, which is shorter than its diff:
```python
import functools

import jax
import jax.numpy as jnp
from jax import lax
from jax.experimental import pallas as pl
from jax.experimental.pallas import tpu as pltpu
from jax.sharding import PartitionSpec as P

INNER_CHANNELS = 3072
EPS_NORM = 1e-05
SUB = 128
NEG = -1e30
BF = jnp.bfloat16
F32 = jnp.float32
HIGHEST = lax.Precision.HIGHEST


def dot_nn(a, b):
    return lax.dot_general(a, b, (((1,), (0,)), ((), ())), preferred_element_type=F32)


def dot_nt(a, b):
    return lax.dot_general(a, b, (((1,), (1,)), ((), ())), preferred_element_type=F32)


def dot_tn(a, b):
    return lax.dot_general(a, b, (((0,), (0,)), ((), ())), preferred_element_type=F32)


def softplus(v):
    return jnp.maximum(v, 0.0) + jnp.log1p(jnp.exp(-jnp.abs(v)))


def lane(shape, dim):
    return lax.broadcasted_iota(jnp.int32, shape, dim)


def wide(column):
    return jnp.broadcast_to(column, (SUB, SUB))


def decays(raw, par_ref):
    rate = par_ref[1:2, :]
    shifted = raw + par_ref[0:1, :]
    dt = softplus(shifted)
    lower = (lane((SUB, SUB), 0) >= lane((SUB, SUB), 1)).astype(F32)
    run = jnp.dot(lower, dt * rate, precision=HIGHEST, preferred_element_type=F32)
    return shifted, dt, rate, run


def scan_forward(
    k, gx, marks_ref, taps_ref, bias_ref, par_ref, skip_ref, gain_ref, down_ref,
    y_ref, xc_ref, bc_ref, slope_ref, g2_ref, states_ref, stats_ref, state, ext,
):
    inner = skip_ref.shape[1]
    chans = ext.shape[1]
    rows = pl.ds(pl.multiple_of(k * SUB, SUB), SUB)

    def strip(ref, at):
        each = ref.shape[2] // SUB
        return ref[at // each, rows, (at % each) * SUB : (at % each + 1) * SUB].astype(F32)

    @pl.when(k == 0)
    def _():
        state[...] = jnp.zeros_like(state)
        ext[0:8, :] = jnp.zeros((8, chans), F32)

    @pl.when(k > 0)
    def _():
        ext[0:8, :] = ext[SUB : SUB + 8, :]

    for c in range(chans // SUB):
        ext[8 : SUB + 8, c * SUB : (c + 1) * SUB] = strip(gx, inner // SUB + c)
    near = [wide(marks_ref[:, k : k + 1]) for k in range(3)]
    linked = wide(marks_ref[:, 3:4])
    ending = wide(marks_ref[:, 4:5])
    ids = wide(marks_ref[:, 5:6])
    passing = marks_ref[0:1, 6:7]
    left = lane((SUB, SUB), 1) < 64

    def conv(sl):
        pre = bias_ref[:, sl] + taps_ref[3:4, sl] * ext[8 : SUB + 8, sl]
        for k in range(1, 4):
            pre = pre + taps_ref[3 - k : 4 - k, sl] * (ext[8 - k : SUB + 8 - k, sl] * near[k - 1])
        sig = jax.nn.sigmoid(pre)
        out = (pre * sig).astype(BF)
        slope_ref[:, sl] = (sig * (1.0 + pre * (1.0 - sig))).astype(BF)
        return out

    b_low = conv(slice(inner, inner + SUB))
    c_low = conv(slice(inner + SUB, inner + 2 * SUB))
    bc_ref[:, 0:SUB] = b_low
    bc_ref[:, SUB : 2 * SUB] = c_low
    b_turned = b_low.astype(F32).T.astype(BF)
    _, dt, _, run = decays(strip(gx, (inner + chans) // SUB), par_ref)
    run_rows = run.T
    allowed = (ids == ids.T) & (lane((SUB, SUB), 0) >= lane((SUB, SUB), 1))
    mask = jnp.where(allowed, 0.0, NEG)
    cross = dot_nt(c_low, b_low)
    square = jnp.zeros((SUB, SUB), F32)
    for p in range(inner // SUB):
        sl = slice(p * SUB, (p + 1) * SUB)
        x_low = conv(sl)
        xc_ref[:, sl] = x_low
        x = x_low.astype(F32)
        run0, run1 = wide(run[:, 2 * p : 2 * p + 1]), wide(run[:, 2 * p + 1 : 2 * p + 2])
        run_p = jnp.where(left, run0, run1)
        dt_p = jnp.where(left, wide(dt[:, 2 * p : 2 * p + 1]), wide(dt[:, 2 * p + 1 : 2 * p + 2]))
        m0 = (jnp.exp(run0 - run_rows[2 * p : 2 * p + 1, :] + mask) * cross).astype(BF)
        m1 = (jnp.exp(run1 - run_rows[2 * p + 1 : 2 * p + 2, :] + mask) * cross).astype(BF)
        xdt = x * dt_p
        split = jnp.concatenate([jnp.where(left, xdt, 0.0), jnp.where(left, 0.0, xdt)], 0).astype(BF)
        before = state[:, sl]
        before_low = before.astype(BF)
        states_ref[0, :, sl] = before_low
        y = dot_nn(jnp.concatenate([m0, m1], 1), split)
        y = y + jnp.exp(run_p) * linked * dot_nn(c_low, before_low) + skip_ref[:, sl] * x
        last = run_p[SUB - 1 : SUB, :]
        toward = (xdt * (jnp.exp(last - run_p) * ending)).astype(BF)
        state[:, sl] = (jnp.exp(last) * passing) * before + dot_nn(b_turned, toward)
        z = strip(gx, p)
        gated = y * (z * jax.nn.sigmoid(z))
        y_ref[:, sl] = y.astype(BF)
        g2_ref[:, sl] = (gated * gain_ref[:, sl]).astype(BF)
        square = square + gated * gated
    stats_ref[0:8, rows] = lane_rows(square)
    stats_ref[8:, rows] = dot_nt(down_ref[...], g2_ref[...])


def forward_all(
    me_ref, p0, p1, p2, p3, p4, norm_gain_ref, down_ref, up_ref, w_ref, w0_ref, w1_ref, out_down_ref,
    marks_ref, taps_ref, bias_ref, par_ref, skip_ref, gain_ref,
    normed_hbm, gx_hbm, rank_t_ref, stats_ref, y_ref, xc_ref, bc_ref, slope_ref, g2_ref, states_ref, out_ref,
    normed, gx, rank, state, ext, g2_all, held, sems,
):
    step = pl.program_id(0)
    tiles, length, tile = gx.shape
    copy_normed = pltpu.make_async_copy(normed, normed_hbm, sems.at[0])

    def copy_gx(j):
        return pltpu.make_async_copy(gx.at[j], gx_hbm.at[:, pl.ds(j * tile, tile)], sems.at[1 + j])

    @pl.when(step == 0)
    def _():
        ordered(me_ref, (p0, p1, p2, p3, p4), down_ref, normed, rank, rank_t_ref, norm_gain_ref)
        copy_normed.start()

    for j in range(tiles):

        @pl.when(step == j)
        def _():
            gx[j] = (dot_nn(normed[...], w_ref[...]) + dot_nn(rank[...], up_ref[...])).astype(BF)
            copy_gx(j).start()

    done = tiles + length // SUB

    @pl.when((step >= tiles) & (step < done))
    def _():
        scan_forward(
            step - tiles, gx, marks_ref, taps_ref, bias_ref, par_ref, skip_ref, gain_ref, out_down_ref,
            y_ref, xc_ref, bc_ref, slope_ref, g2_ref, states_ref, stats_ref, state, ext,
        )
        g2_all[pl.ds(pl.multiple_of((step - tiles) * SUB, SUB), SUB), :] = g2_ref[...]

    @pl.when(step >= done)
    def _():
        cut = w0_ref.shape[1]
        held[...] = (dot_nt(g2_all[:, 0:cut], w0_ref[...]) + dot_nt(g2_all[:, cut:], w1_ref[...])).astype(BF)
        owners, rows, _ = out_ref.shape
        share = 64
        for c in range(rows // share):
            for y in range(owners):
                at = (c * owners + y) * share
                out_ref[y, c * share : (c + 1) * share, :] = held[at : at + share, :]

    @pl.when(step == pl.num_programs(0) - 1)
    def _():
        copy_normed.wait()
        for j in range(tiles):
            copy_gx(j).wait()


def backward_half(
    me_ref, z_ref, dt_ref, xc_ref, bc_ref, slope_ref, y_ref, dn_ref, states_ref, s0_ref, s1_ref, s2_ref, s3_ref, marks_ref,
    taps_ref, par_ref, skip_ref, gain_ref, pick_ref, lam_in_ref, edge_in_ref,
    w_ref, down_ref, up_ref, rank_t_ref, *rest, with_grads,
):
    if with_grads:
        (cot0_ref, g20_ref, low0_ref, cot1_ref, g21_ref, low1_ref, q0_ref, q1_ref, q2_ref, q3_ref), rest = rest[:10], rest[10:]
        o0, o1, o2, o3, lam, edge_ref, up_grad_ref, grads_ref, *scratch = rest
        grads, *scratch = scratch
    else:
        o0, o1, o2, o3, lam, edge_ref, up_grad_ref, *scratch = rest
    d_all, low, pushed, held, ext, to_dt, to_run, to_end = scratch
    step = pl.program_id(0)
    steps = d_all.shape[0] // SUB
    if with_grads:

        @pl.when(step == 0)
        def _():
            grads[...] = jnp.zeros_like(grads)

        @pl.when(step < steps)
        def _():
            cut = g20_ref.shape[1]
            for stats, low_t_ref, cot_ref, g2_ref in (
                (s0_ref[...] + s1_ref[...] + s2_ref[...] + s3_ref[...], low0_ref, cot0_ref, g20_ref),
                (q0_ref[...] + q1_ref[...] + q2_ref[...] + q3_ref[...], low1_ref, cot1_ref, g21_ref),
            ):
                rn_row = lax.rsqrt(stats[0:1, :] / INNER_CHANNELS + EPS_NORM)
                grads[:, 0:cut] += dot_nn((low_t_ref[...].astype(F32) * rn_row).astype(BF), g2_ref[...])
                grads[:, cut:] += dot_nn((stats[8:, :] * rn_row).astype(BF), cot_ref[...])

        @pl.when(step == steps)
        def _():
            grads_ref[...] = grads[...].astype(BF)

    @pl.when(step < steps)
    def _():
        at = pl.multiple_of((steps - 1 - step) * SUB, SUB)
        scan_backward(
            step, d_all.at[pl.ds(at, SUB), :], z_ref, dt_ref, xc_ref, bc_ref, slope_ref, y_ref, dn_ref, states_ref,
            (s0_ref, s1_ref, s2_ref, s3_ref), marks_ref, taps_ref, par_ref, skip_ref, gain_ref, pick_ref, lam_in_ref, edge_in_ref,
            lam, ext, to_dt, to_run, to_end,
        )
        gate = d_all[pl.ds(at, SUB), 0 : up_ref.shape[1]]
        part = dot_nt(gate, up_ref[...])
        rank = part.shape[1]
        low[pl.ds(at, SUB), :] = part.astype(BF)
        part = jnp.concatenate([part, jnp.zeros((SUB, SUB - rank), F32)], 1)
        pushed[:, pl.ds(at, SUB)] = part.T[0:rank, :].astype(BF)
        up_grad = dot_nn(rank_t_ref[...], gate)

        @pl.when(step == 0)
        def _():
            up_grad_ref[...] = up_grad

        @pl.when(step > 0)
        def _():
            up_grad_ref[...] += up_grad

    @pl.when(step == steps - 1)
    def _():
        edge_ref[...] = ext[0:8, :]

    @pl.when(step >= steps)
    def _():
        held[...] = (dot_nt(d_all[...], w_ref[...]) + dot_nn(low[...], down_ref[...])).astype(BF)
        deal(me_ref[0], held, (o0, o1, o2, o3))

    for out in (o0, o1, o2, o3):

        @pl.when(step == steps)
        def _():
            out[out.shape[0] - pushed.shape[0] :, :] = pushed[...]

        @pl.when(step > steps)
        def _():
            out[out.shape[0] - pushed.shape[0] :, :] = jnp.zeros_like(pushed)


def scan_backward(
    step, da_ref, z_ref, dt_ref, xc_ref, bc_ref, slope_ref, y_ref, dn_ref, states_ref, stats_refs, marks_ref,
    taps_ref, par_ref, skip_ref, gain_ref, pick_ref, lam_in_ref, edge_in_ref,
    lam, ext, to_dt, to_run, to_end,
):
    inner = z_ref.shape[1]
    chans = ext.shape[1]

    @pl.when(step == 0)
    def _():
        lam[...] = lam_in_ref[...]
        ext[SUB : SUB + 8, :] = edge_in_ref[...]

    @pl.when(step > 0)
    def _():
        ext[SUB : SUB + 8, :] = ext[0:8, :]

    linked = wide(marks_ref[:, 3:4])
    ending = wide(marks_ref[:, 4:5])
    ids = wide(marks_ref[:, 5:6])
    passing = marks_ref[0:1, 6:7]
    later = [wide(marks_ref[:, 7 + k : 8 + k]) for k in range(3)]
    left = lane((SUB, SUB), 1) < 64
    stats = stats_refs[0][...] + stats_refs[1][...] + stats_refs[2][...] + stats_refs[3][...]
    rn_row = lax.rsqrt(stats[0:1, :] / INNER_CHANNELS + EPS_NORM)
    rn = jnp.broadcast_to(rn_row, (SUB, SUB)).T
    kappa = jnp.broadcast_to(rn_row * rn_row * rn_row * stats[1:2, :] / INNER_CHANNELS, (SUB, SUB)).T
    shifted, dt, rate, run = decays(dt_ref[...].astype(F32), par_ref)
    run_rows = run.T
    b_low, c_low = bc_ref[:, 0:SUB], bc_ref[:, SUB : 2 * SUB]
    c_turned = c_low.astype(F32).T.astype(BF)
    allowed = (ids == ids.T) & (lane((SUB, SUB), 0) <= lane((SUB, SUB), 1))
    mask = jnp.where(allowed, 0.0, NEG)
    cross = dot_nt(b_low, c_low)
    d_cross = jnp.zeros((SUB, SUB), F32)
    d_b = jnp.zeros((SUB, SUB), F32)
    d_c = jnp.zeros((SUB, SUB), F32)
    for p in range(inner // SUB):
        sl = slice(p * SUB, (p + 1) * SUB)
        z = z_ref[:, sl].astype(F32)
        sig = jax.nn.sigmoid(z)
        silu = z * sig
        y = y_ref[:, sl].astype(F32)
        d_gated = rn * (dn_ref[:, sl].astype(F32) * gain_ref[:, sl]) - kappa * (y * silu)
        da_ref[:, sl] = (d_gated * y * sig * (1.0 + z * (1.0 - sig))).astype(BF)
        dy = d_gated * silu
        x = xc_ref[:, sl].astype(F32)
        run0, run1 = wide(run[:, 2 * p : 2 * p + 1]), wide(run[:, 2 * p + 1 : 2 * p + 2])
        run_p = jnp.where(left, run0, run1)
        dt_p = jnp.where(left, wide(dt[:, 2 * p : 2 * p + 1]), wide(dt[:, 2 * p + 1 : 2 * p + 2]))
        l0 = jnp.exp(run_rows[2 * p : 2 * p + 1, :] - run0 + mask)
        l1 = jnp.exp(run_rows[2 * p + 1 : 2 * p + 2, :] - run1 + mask)
        xdt = x * dt_p
        x_split = jnp.concatenate([jnp.where(left, xdt, 0.0), jnp.where(left, 0.0, xdt)], 0).astype(BF)
        dy_split = jnp.concatenate([jnp.where(left, dy, 0.0), jnp.where(left, 0.0, dy)], 0).astype(BF)
        d_m = dot_nt(x_split, dy.astype(BF))
        d_cross = d_cross + l0 * d_m[0:SUB] + l1 * d_m[SUB : 2 * SUB]
        m = jnp.concatenate([l0 * cross, l1 * cross], 1).astype(BF)
        lam_p = lam[:, sl]
        lam_low = lam_p.astype(BF)
        last = run_p[SUB - 1 : SUB, :]
        toward = jnp.exp(last - run_p) * ending
        carried = toward * dot_nn(b_low, lam_low)
        d_xt = dot_nn(m, dy_split) + carried
        skip = skip_ref[:, sl]
        ext[0:SUB, sl] = (dt_p * d_xt + skip * dy) * slope_ref[:, sl].astype(F32)
        x_dx = x * d_xt
        to_dt[:, sl] = x_dx
        to_run[:, sl] = dy * (y - skip * x) - dt_p * x_dx
        reached = (jnp.exp(run_p) * linked * dy).astype(BF)
        before_low = states_ref[0, :, sl]
        keep = jnp.exp(last) * passing
        to_end[0:1, sl] = jnp.sum(xdt * carried, 0, keepdims=True) + keep * jnp.sum(
            lam_p * before_low.astype(F32), 0, keepdims=True
        )
        d_b = d_b + dot_nt((xdt * toward).astype(BF), lam_low)
        d_c = d_c + dot_nt(reached, before_low)
        lam[:, sl] = keep * lam_p + dot_nn(c_turned, reached)
    d_cross_low = d_cross.astype(BF)
    d_b = d_b + dot_nn(d_cross_low, c_low)
    d_c = d_c + dot_nn(d_cross.T.astype(BF), b_low)
    ext[0:SUB, inner : inner + SUB] = d_b * slope_ref[:, inner : inner + SUB].astype(F32)
    ext[0:SUB, inner + SUB : chans] = d_c * slope_ref[:, inner + SUB : chans].astype(F32)

    def by_head(v):
        high = v.astype(BF)
        return dot_nn(high, pick_ref[...]) + dot_nn((v - high.astype(F32)).astype(BF), pick_ref[...])

    d_run = by_head(to_run[...])
    d_end = by_head(to_end[...])[0:1, :]
    d_run = d_run + jnp.where(lane((SUB, SUB), 0) == SUB - 1, d_end, 0.0)
    upper = (lane((SUB, SUB), 0) <= lane((SUB, SUB), 1)).astype(F32)
    d_log = jnp.dot(upper, d_run, precision=HIGHEST, preferred_element_type=F32)
    d_dt = by_head(to_dt[...]) + rate * d_log
    da_ref[:, inner + chans : inner + chans + SUB] = (d_dt * jax.nn.sigmoid(shifted)).astype(BF)
    for s in range(chans // SUB):
        sl = slice(s * SUB, (s + 1) * SUB)
        acc = taps_ref[3:4, sl] * ext[0:SUB, sl]
        for k in range(1, 4):
            acc = acc + taps_ref[3 - k : 4 - k, sl] * (ext[k : SUB + k, sl] * later[k - 1])
        da_ref[:, inner + s * SUB : inner + (s + 1) * SUB] = acc.astype(BF)

def whole(a):
    return pl.BlockSpec(a.shape, lambda i, *_: (0,) * a.ndim)


def params(mib=60):
    return pltpu.CompilerParams(vmem_limit_bytes=mib << 20)


def takes(us):
    return pl.CostEstimate(flops=us * 100_000_000, bytes_accessed=us * 300_000, transcendentals=0)


def assemble(me, pieces, out_ref, block):
    own, behind, ahead, far_low, far_high = pieces
    chunks, share = own.shape[0], own.shape[1]
    for c in range(chunks):
        far = far_low[c] if c < chunks // 2 else far_high[c - chunks // 2]
        for d, part in ((0, own[c]), (1, behind[c]), (2, far), (3, ahead[c])):
            at = pl.multiple_of(c * block + ((me + 4 - d) % 4) * share, share)
            out_ref[pl.ds(at, share), :] = part


def low_products(rows_ref, down_ref, rank_ref, rank_t_ref):
    low = dot_nt(rows_ref[...], down_ref[...])
    rank = low.shape[1]
    rank_ref[...] = low.astype(BF)
    low = jnp.concatenate([low, jnp.zeros((low.shape[0], SUB - rank), F32)], 1)
    for k in range(low.shape[0] // SUB):
        here = slice(k * SUB, (k + 1) * SUB)
        rank_t_ref[:, here] = low[here, :].T[0:rank, :].astype(BF)


def ordered(me_ref, pieces, down_ref, rows_ref, rank_ref, rank_t_ref, gain_ref):
    assemble(me_ref[0], pieces, rows_ref, 4 * pieces[0].shape[1])
    for k in range(rows_ref.shape[0] // 64):
        here = slice(k * 64, (k + 1) * 64)
        t = rows_ref[here, :].astype(F32)
        rms = lax.rsqrt(jnp.mean(t * t, -1, keepdims=True) + EPS_NORM)
        rows_ref[here, :] = (t * rms * gain_ref[...]).astype(BF)
    low_products(rows_ref, down_ref, rank_ref, rank_t_ref)


def lane_rows(v):
    return lax.dot_general(
        jnp.ones((8, v.shape[1]), F32), v, (((1,), (1,)), ((), ())), precision=HIGHEST, preferred_element_type=F32
    )


def deal(me, held, outs):
    share = 64
    for c in range(held.shape[0] // (4 * share)):
        for d, out in enumerate(outs):
            at = pl.multiple_of((c * 4 + (me + d) % 4) * share, share)
            out[c * share : (c + 1) * share, :] = held[pl.ds(at, share), :]


def one(a):
    return pl.BlockSpec(a.shape, lambda i, *_: (0,) * a.ndim, pipeline_mode=pl.Buffered(1))


def kept(*shape):
    return pl.BlockSpec(shape, lambda i, *_: (0,) * len(shape))


def run_forward(me, pieces, norm_gain, down, up, weights, out_down, marks, taps, bias, par, skip, gain):
    chunks, share, width = pieces[0].shape
    length = chunks * 4 * share
    inner, chans = skip.shape[1], taps.shape[1]
    rank, columns = up.shape
    tile = 512
    tiles, steps, out_tiles = columns // tile, length // SUB, width // tile
    any_space = pl.BlockSpec(memory_space=pl.ANY)
    sub = lambda i: jnp.clip(i - tiles, 0, steps - 1)
    scan = lambda cols: pl.BlockSpec((SUB, cols), lambda i, me: (sub(i), 0))
    last = lambda i: jnp.maximum(i - tiles - steps, 0)
    at_out = 2 * (weights.shape[1] - inner) // inner
    return pl.pallas_call(
        forward_all,
        grid_spec=pltpu.PrefetchScalarGridSpec(
            num_scalar_prefetch=1,
            grid=(tiles + steps + out_tiles,),
            in_specs=[
                *[one(p) for p in pieces], one(norm_gain), one(down),
                pl.BlockSpec((rank, tile), lambda i, me: (0, jnp.minimum(i, tiles - 1))),
                pl.BlockSpec((width, tile), lambda i, me: (0, jnp.minimum(i, tiles - 1))),
                pl.BlockSpec((tile, inner // 2), lambda i, me: (last(i), at_out)),
                pl.BlockSpec((tile, inner // 2), lambda i, me: (last(i), at_out + 1)),
                one(out_down), scan(marks.shape[1]), one(taps), one(bias), one(par), one(skip), one(gain),
            ],
            out_specs=[
                any_space, any_space, kept(rank, length), kept(8 + rank, length),
                scan(inner), scan(inner), scan(2 * SUB), scan(chans), scan(inner),
                pl.BlockSpec((1, SUB, inner), lambda i, me: (sub(i), 0, 0)),
                pl.BlockSpec((4, length // 4, tile), lambda i, me: (0, 0, last(i))),
            ],
            scratch_shapes=[
                pltpu.VMEM((length, width), BF),
                pltpu.VMEM((tiles, length, tile), BF),
                pltpu.VMEM((length, rank), BF),
                pltpu.VMEM((SUB, inner), F32),
                pltpu.VMEM((SUB + 8, chans), F32),
                pltpu.VMEM((length, inner), BF),
                pltpu.VMEM((length, tile), BF),
                pltpu.SemaphoreType.DMA((1 + tiles,)),
            ],
        ),
        out_shape=[
            jax.ShapeDtypeStruct((length, width), BF),
            jax.ShapeDtypeStruct((length, columns), BF),
            jax.ShapeDtypeStruct((rank, length), BF),
            jax.ShapeDtypeStruct((8 + rank, length), F32),
            jax.ShapeDtypeStruct((length, inner), BF),
            jax.ShapeDtypeStruct((length, inner), BF),
            jax.ShapeDtypeStruct((length, 2 * SUB), BF),
            jax.ShapeDtypeStruct((length, chans), BF),
            jax.ShapeDtypeStruct((length, inner), BF),
            jax.ShapeDtypeStruct((steps, SUB, inner), BF),
            jax.ShapeDtypeStruct((4, length // 4, width), BF),
        ],
        compiler_params=params(),
        cost_estimate=takes(30),
        name="forward_all",
    )(me, *pieces, norm_gain, down, up, weights, weights, weights, out_down, marks, taps, bias, par, skip, gain)


def pull_back(
    me_ref, p0, p1, p2, p3, up_ref, w_ref, g2_ref, part_ref, down_ref,
    dn_ref, stats_ref, cot_hbm, low_t_ref,
    cot, low, dots, sem,
):
    step = pl.program_id(0)
    copy_cot = pltpu.make_async_copy(cot, cot_hbm, sem)

    @pl.when(step == 0)
    def _():
        chunks, share, _ = p0.shape
        for c in range(chunks):
            for d, part in enumerate((p0, p1, p2, p3)):
                at = pl.multiple_of((c * 4 + (me_ref[0] + 4 - d) % 4) * share, share)
                cot[pl.ds(at, share), :] = part[(me_ref[1] + 4 - c) % 4]
        copy_cot.start()
        low_products(cot, up_ref, low, low_t_ref)
        dots[...] = jnp.zeros_like(dots)

    dn = dot_nn(cot[...], w_ref[...]) + dot_nn(low[...], down_ref[...])
    dn_ref[...] = dn.astype(BF)
    both = dn * g2_ref[...].astype(F32)
    total = dots[...]
    for k in range(both.shape[1] // SUB):
        total = total + both[:, k * SUB : (k + 1) * SUB]
    dots[...] = total

    @pl.when(step == pl.num_programs(0) - 1)
    def _():
        first = lane((8, stats_ref.shape[1]), 0) == 0
        stats_ref[0:8, :] = jnp.where(first, part_ref[0:8, :], lane_rows(dots[...]))
        stats_ref[8:, :] = part_ref[8:, :]
        copy_cot.wait()


def run_pull_back(me, pieces, weights, up, g2, part, down, tile=384):
    width = pieces[0].shape[2]
    length, inner = g2.shape
    rank = down.shape[0]
    first = (weights.shape[1] - inner) // tile
    return pl.pallas_call(
        pull_back,
        grid_spec=pltpu.PrefetchScalarGridSpec(
            num_scalar_prefetch=1,
            grid=(inner // tile,),
            in_specs=[
                *[one(p) for p in pieces], one(up),
                pl.BlockSpec((width, tile), lambda j, me: (0, first + j)),
                pl.BlockSpec((length, tile), lambda j, me: (0, j)),
                one(part),
                pl.BlockSpec((rank, tile), lambda j, me: (0, j)),
            ],
            out_specs=[
                pl.BlockSpec((length, tile), lambda j, me: (0, j)), kept(*part.shape),
                pl.BlockSpec(memory_space=pl.ANY), kept(rank, length),
            ],
            scratch_shapes=[
                pltpu.VMEM((length, width), BF),
                pltpu.VMEM((length, rank), BF),
                pltpu.VMEM((length, SUB), F32),
                pltpu.SemaphoreType.DMA,
            ],
        ),
        out_shape=[
            jax.ShapeDtypeStruct((length, inner), BF),
            jax.ShapeDtypeStruct(part.shape, F32),
            jax.ShapeDtypeStruct((length, width), BF),
            jax.ShapeDtypeStruct((rank, length), BF),
        ],
        compiler_params=params(),
        cost_estimate=takes(8),
        name="pull_back",
    )(me, *pieces, up, weights, g2, part, down)


def dealt(rows, width, tile, at):
    spec = pl.BlockSpec((rows, tile), lambda j, me: (0, at(j)))
    return [spec] * 4, [jax.ShapeDtypeStruct((rows, width), BF)] * 4


def run_backward(
    me, half, gx, xc, bc, slope, y, dn, states, stats, marks, taps, par, skip, gain, pick,
    weights, down, up, rank_t, lam, edge, cot=None, g2=None, low_t=None,
):
    length = gx.shape[0] // 2
    inner, chans, width = skip.shape[1], taps.shape[1], weights.shape[0]
    rank = down.shape[0]
    steps = length // SUB
    tile = 512
    assert tile == length
    top = (half + 1) * steps - 1
    sub = lambda i: jnp.maximum(top - i, half * steps)
    col = lambda i: jnp.maximum(i - steps, 0)
    row = lambda cols, at=0: pl.BlockSpec((SUB, cols), lambda i, me, at=at: (sub(i), at))
    lanes = lambda n: pl.BlockSpec((n, SUB), lambda i, me: (0, sub(i)))
    total = inner + chans + SUB
    specs, shapes = dealt(length // 4 + rank, width, tile, col)
    with_grads = cot is not None
    args = [
        gx, gx, xc, bc, slope, y, dn, states, *stats, marks, taps, par, skip, gain, pick, lam, edge,
        weights, down, up, rank_t,
    ]
    in_specs = [
        row(inner), row(SUB, (inner + chans) // SUB), row(inner), row(2 * SUB), row(chans), row(inner), row(inner),
        pl.BlockSpec((1, SUB, inner), lambda i, me: (sub(i), 0, 0)),
        *[lanes(stats[0].shape[0])] * 4,
        row(marks.shape[1]), one(taps), one(par), one(skip), one(gain), one(pick), one(lam), one(edge),
        pl.BlockSpec((tile, total), lambda i, me: (col(i), 0)),
        pl.BlockSpec((rank, tile), lambda i, me: (0, col(i))),
        one(up), lanes(rank),
    ]
    out_specs = [*specs, kept(*lam.shape), kept(*edge.shape), kept(*up.shape)]
    out_shape = [
        *shapes,
        jax.ShapeDtypeStruct(lam.shape, F32),
        jax.ShapeDtypeStruct(edge.shape, F32),
        jax.ShapeDtypeStruct(up.shape, F32),
    ]
    scratch = [
        pltpu.VMEM((length, total), BF),
        pltpu.VMEM((length, rank), BF),
        pltpu.VMEM((rank, length), BF),
        pltpu.VMEM((length, tile), BF),
        pltpu.VMEM((SUB + 8, chans), F32),
        pltpu.VMEM((SUB, inner), F32),
        pltpu.VMEM((SUB, inner), F32),
        pltpu.VMEM((8, inner), F32),
    ]
    if with_grads:
        other = lambda i: sub(i) - steps
        args += [cot, g2, low_t, cot, g2, low_t, *stats]
        in_specs += [row(width), row(inner), lanes(rank)]
        in_specs += [
            pl.BlockSpec((SUB, width), lambda i, me: (other(i), 0)),
            pl.BlockSpec((SUB, inner), lambda i, me: (other(i), 0)),
            pl.BlockSpec((rank, SUB), lambda i, me: (0, other(i))),
            *[pl.BlockSpec((stats[0].shape[0], SUB), lambda i, me: (0, other(i)))] * 4,
        ]
        out_specs.append(kept(rank, inner + width))
        out_shape.append(jax.ShapeDtypeStruct((rank, inner + width), BF))
        scratch = [pltpu.VMEM((rank, inner + width), F32), *scratch]
    return pl.pallas_call(
        functools.partial(backward_half, with_grads=with_grads),
        grid_spec=pltpu.PrefetchScalarGridSpec(
            num_scalar_prefetch=1,
            grid=(steps + width // tile,),
            in_specs=in_specs,
            out_specs=out_specs,
            scratch_shapes=scratch,
        ),
        out_shape=out_shape,
        compiler_params=params(),
        cost_estimate=takes(19),
        name="backward_half",
    )(me, *args)


def place(me_ref, pieces, out):
    own, behind, ahead, far_low, far_high = pieces
    share = own.shape[1]
    y, turn = me_ref[0], (me_ref[1] + 4 - pl.program_id(0)) % 4
    for d, part in ((0, own), (1, behind), (3, ahead)):
        out[pl.ds(pl.multiple_of(((y + 4 - d) % 4) * share, share), share), :] = part[0]
    far = pl.ds(pl.multiple_of(((y + 2) % 4) * share, share), share)

    @pl.when(turn < 2)
    def _():
        out[far, :] = far_low[0]

    @pl.when(turn >= 2)
    def _():
        out[far, :] = far_high[0]


def columns_of(stats_refs, cols):
    total = stats_refs[0][...] + stats_refs[1][...] + stats_refs[2][...] + stats_refs[3][...]
    rows, length = total.shape
    total = jnp.concatenate([total, jnp.zeros((SUB - rows, length), F32)], 0)
    for k in range(length // SUB):
        cols[k * SUB : (k + 1) * SUB, :] = total[:, k * SUB : (k + 1) * SUB].T
    return total


def finish_branch(me_ref, sum_ref, s0, s1, s2, s3, up_ref, o0, o1, o2, o3, cols):
    columns_of((s0, s1, s2, s3), cols)
    share = o0.shape[0]
    rank = up_ref.shape[0]
    for d, out in enumerate((o0, o1, o2, o3)):
        c = (me_ref[1] + d) % 4
        mine = cols[pl.ds(pl.multiple_of((c * 4 + me_ref[0]) * share, share), share), :]
        rn = lax.rsqrt(mine[:, 0:1] / INNER_CHANNELS + EPS_NORM)
        low = (mine[:, 8 : 8 + rank] * rn).astype(BF)
        total = sum_ref[pl.ds(pl.multiple_of(c * share, share), share), :].astype(F32)
        out[...] = (total * rn + dot_nn(low, up_ref[...])).astype(BF)


def run_to_context(kernel, me, args, share, width, scratch, name):
    return pl.pallas_call(
        kernel,
        grid_spec=pltpu.PrefetchScalarGridSpec(
            num_scalar_prefetch=1,
            grid=(1,),
            in_specs=[one(a) for a in args],
            out_specs=[kept(share, width)] * 4,
            scratch_shapes=[scratch],
        ),
        out_shape=[jax.ShapeDtypeStruct((share, width), BF)] * 4,
        compiler_params=params(),
        cost_estimate=takes(3),
        name=name,
    )(me, *args)


def in_grads(me_ref, *refs):
    early, late, (up0_ref, up1_ref, normed_ref, done_ref), outs, (sent_ref, held) = (
        refs[:4], refs[4:8], refs[8:12], refs[12:16], refs[16:]
    )
    half = held.shape[0] // 2
    rank, length = up0_ref.shape[0], normed_ref.shape[0]
    added = lambda refs, *at: sum(r[at].astype(F32) for r in refs[1:]) + refs[0][at].astype(F32)
    for at, parts in ((0, early), (half, late)):
        held[at : at + half, :] = added(parts, slice(0, half)).astype(BF)
    share = outs[0].shape[0]
    for d, out in enumerate(outs):
        c = (me_ref[1] + d) % 4
        out[...] = held[pl.ds(pl.multiple_of(c * share, share), share), :]
    ranks = [added(parts, slice(half, half + rank), slice(0, length // 2)) for parts in (early, late)]
    width, inner2, done = normed_ref.shape[1], up0_ref.shape[1], done_ref.shape[1]
    sent_ref[:, 0:width] = dot_nn(jnp.concatenate(ranks, 1).astype(BF), normed_ref[...]).astype(BF)
    sent_ref[:, width : width + inner2] = (up0_ref[...] + up1_ref[...]).astype(BF)
    sent_ref[:, width + inner2 : width + inner2 + done] = done_ref[...]
    sent_ref[:, width + inner2 + done :] = (lane((rank, SUB), 1) == me_ref[2]).astype(BF)


def run_in_grads(me, early, late, up0, up1, normed, done, share):
    rank, inner2 = up0.shape
    width = normed.shape[1]
    columns = width + inner2 + done.shape[1] + SUB
    args = (*early, *late, up0, up1, normed, done)
    return pl.pallas_call(
        in_grads,
        grid_spec=pltpu.PrefetchScalarGridSpec(
            num_scalar_prefetch=1,
            grid=(1,),
            in_specs=[one(a) for a in args],
            out_specs=[*[kept(share, width)] * 4, kept(rank, columns)],
            scratch_shapes=[pltpu.VMEM((4 * share, width), BF)],
        ),
        out_shape=[*[jax.ShapeDtypeStruct((share, width), BF)] * 4, jax.ShapeDtypeStruct((rank, columns), BF)],
        compiler_params=params(),
        cost_estimate=takes(3),
        name="in_grads",
    )(me, *args)


def finish_out(me_ref, p0, p1, p2, p3, p4, tokens_ref, out_ref, held):
    place(me_ref, (p0, p1, p2, p3, p4), held)
    out_ref[0] = (tokens_ref[0].astype(F32) + held[...].astype(F32)).astype(BF)


def finish_grad(me_ref, p0, p1, p2, p3, p4, tokens_ref, cot_ref, gain_ref, out_ref, held):
    place(me_ref, (p0, p1, p2, p3, p4), held)
    t = tokens_ref[0].astype(F32)
    rms = lax.rsqrt(jnp.mean(t * t, -1, keepdims=True) + EPS_NORM)
    pulled = held[...].astype(F32) * gain_ref[...]
    slope = rms * rms * rms * jnp.mean(pulled * t, -1, keepdims=True)
    out_ref[0] = rms * pulled - t * slope + cot_ref[0].astype(F32)


def piece_specs(pieces):
    share, width = pieces[0].shape[1:]
    half = pieces[0].shape[0] // 2
    turn = lambda s, me: (me[1] + 4 - s) % 4
    full = pl.BlockSpec((1, share, width), lambda s, me: (turn(s, me), 0, 0))
    return [
        full, full, full,
        pl.BlockSpec((1, share, width), lambda s, me: (jnp.minimum(turn(s, me), half - 1), 0, 0)),
        pl.BlockSpec((1, share, width), lambda s, me: (jnp.maximum(turn(s, me) - half, 0), 0, 0)),
    ]


def run_finish(kernel, me, pieces, extra, dtype, name):
    seqs, block, width = extra[0].shape
    seq = pl.BlockSpec((1, block, width), lambda s, me: (s, 0, 0))
    specs = [seq if a.ndim == 3 else whole(a) for a in extra]
    return pl.pallas_call(
        kernel,
        grid_spec=pltpu.PrefetchScalarGridSpec(
            num_scalar_prefetch=1,
            grid=(seqs,),
            in_specs=[*piece_specs(pieces), *specs],
            out_specs=seq,
            scratch_shapes=[pltpu.VMEM((block, width), BF)],
        ),
        out_shape=jax.ShapeDtypeStruct((seqs, block, width), dtype),
        compiler_params=params(30),
        cost_estimate=takes(5),
        name=name,
    )(me, *[pltpu.with_memory_space_constraint(a, pltpu.HBM) if a.ndim == 3 else a for a in (*pieces, *extra)])


def fill_tables(all_ref, *outs):
    table, rank = outs[0].shape[0], outs[0].shape[1]
    rows, columns = all_ref.shape
    spread = (lane((SUB, table * rank), 0) == lane((SUB, table * rank), 1) // rank).astype(BF)
    place = dot_nn(all_ref[:, columns - SUB :], spread)
    same = lane((rows, table * rank), 0) % rank == lane((rows, table * rank), 1) % rank
    place = jnp.where(same, place, 0.0).T.astype(BF)
    at = 0
    for out in outs:
        slots = out.shape[2:-1] or (1,)
        for slot in range(slots[0]):
            here = dot_nn(place, all_ref[:, at : at + out.shape[-1]])
            for a in range(table):
                if out.ndim == 3:
                    out[a] = here[a * rank : (a + 1) * rank, :]
                else:
                    out[a, :, slot, :] = here[a * rank : (a + 1) * rank, :]
            at += out.shape[-1]


def run_tables(everything, table, rank, widths):
    return pl.pallas_call(
        fill_tables,
        out_shape=[jax.ShapeDtypeStruct((table, rank, *w), F32) for w in widths],
        compiler_params=params(),
        cost_estimate=takes(3),
        name="fill_tables",
    )(everything)


def shifted_by(value, axis, distance):
    size = lax.axis_size(axis)
    return lax.ppermute(value, axis, [(i, (i + distance) % size) for i in range(size)])


def tie(*values):
    return lax.optimization_barrier(values)


def ring_near(own, axis):
    return shifted_by(own, axis, 1), shifted_by(own, axis, -1)


def ring_far(near, axis):
    half = near[0].shape[0] // 2
    return shifted_by(near[0][:half], axis, 1), shifted_by(near[1][half:], axis, -1)


def delivered(pieces, axis):
    return [pieces[0]] + [shifted_by(p, axis, d) for d, p in enumerate(pieces) if d]


def added(parts):
    return sum(p.astype(F32) for p in parts[1:]) + parts[0].astype(F32)


def shared(value, axis):
    return [value] + [shifted_by(value, axis, d) for d in range(1, lax.axis_size(axis))]


def swapped(value, axis):
    return lax.all_to_all(value, axis, 0, 0, tiled=True)


def per_device(
    tokens, output_cotangent, segments, sequence_adapter, input_norm_gain,
    gate_x_projection_weight, bc_projection_weight, step_projection_weight,
    x_convolution_taps, x_convolution_bias, bc_convolution_taps, bc_convolution_bias,
    step_size_bias, log_decay_rate, head_skip_gain, gated_norm_gain, output_projection_weight,
    in_adapter_down, in_adapter_up, out_adapter_down, out_adapter_up,
):
    seqs, block, width = tokens.shape
    inner = gate_x_projection_weight.shape[2]
    heads = step_projection_weight.shape[1]
    rank = in_adapter_down.shape[2]
    ny, nz = lax.axis_size("tensor"), lax.axis_size("context")
    my, mz = lax.axis_index("tensor"), lax.axis_index("context")
    me = jnp.stack([my, mz]).astype(jnp.int32)
    length = block * nz
    share = block // ny

    rows = gate_x_projection_weight.shape[0]
    packed = jnp.concatenate(
        [
            gate_x_projection_weight.reshape(rows, 2 * inner),
            bc_projection_weight,
            step_projection_weight,
            jnp.zeros((rows, SUB - heads), BF),
            output_projection_weight.T,
        ],
        1,
    )
    full = lax.all_gather(packed, ("fsdp", "context"), axis=0, tiled=True)

    quarter = lambda a: lax.dynamic_slice_in_dim(a, my * share, share, 1)
    tokens_q = quarter(tokens)
    later = (
        segments, sequence_adapter, x_convolution_taps, x_convolution_bias, bc_convolution_taps, bc_convolution_bias,
        step_size_bias, log_decay_rate, head_skip_gain, gated_norm_gain,
        in_adapter_down, in_adapter_up, out_adapter_down, out_adapter_up,
    )
    tokens_s, cot_later, later = tie(swapped(tokens_q, "context"), output_cotangent, later)
    cot_q = [
        lax.dynamic_slice(cot_later, ((mz + d) % nz, my * share, 0), (1, share, width)) for d in range(nz)
    ]
    (
        segments, sequence_adapter, x_convolution_taps, x_convolution_bias, bc_convolution_taps, bc_convolution_bias,
        step_size_bias, log_decay_rate, head_skip_gain, gated_norm_gain,
        in_adapter_down, in_adapter_up, out_adapter_down, out_adapter_up,
    ) = later
    tokens_near = ring_near(tokens_s, "tensor")

    seg = swapped(segments, "context").reshape(length)
    mine = lax.dynamic_index_in_dim(sequence_adapter, mz, 0, False)
    down_in = lax.dynamic_index_in_dim(in_adapter_down.transpose(0, 2, 1), mine, 0, False)
    up_in = lax.dynamic_index_in_dim(in_adapter_up, mine, 0, False).reshape(rank, 2 * inner)
    down_out = lax.dynamic_index_in_dim(out_adapter_down.transpose(0, 2, 1), mine, 0, False)
    up_out = lax.dynamic_index_in_dim(out_adapter_up, mine, 0, False)

    pos = jnp.arange(length)
    by_sub = seg.reshape(-1, SUB)
    last = by_sub[:, -1]
    before = jnp.concatenate([jnp.full((1,), -1, seg.dtype), last[:-1]])
    back = [jnp.where(pos >= k, jnp.roll(seg, k) == seg, False) for k in (1, 2, 3)]
    forth = [jnp.where(pos < length - k, jnp.roll(seg, -k) == seg, False) for k in (1, 2, 3)]
    same = lambda v: jnp.broadcast_to(v[:, None], by_sub.shape)
    kinds = [
        *back,
        (by_sub == same(before)).reshape(-1),
        (by_sub == same(last)).reshape(-1),
        seg,
        same(last == before).reshape(-1),
        *forth,
    ]
    marks = jnp.stack([c.astype(F32) for c in kinds] + [jnp.zeros((length,), F32)] * 6, -1)

    taps = jnp.concatenate([x_convolution_taps, bc_convolution_taps], 1)
    conv_bias = jnp.concatenate([x_convolution_bias, bc_convolution_bias], 0)[None]
    par = jnp.zeros((8, SUB), F32)
    par = par.at[0, :heads].set(step_size_bias).at[1, :heads].set(-jnp.exp(log_decay_rate))
    skip = jnp.repeat(head_skip_gain, inner // heads)[None]
    gain = gated_norm_gain[None]
    pick = (jnp.arange(inner)[:, None] // (inner // heads) == jnp.arange(SUB)[None, :]).astype(BF)

    up_wide = jnp.pad(up_in, ((0, 0), (0, 512)))
    lam, edge = jnp.zeros((SUB, inner), F32), jnp.zeros((8, taps.shape[1]), F32)
    mine = mine.reshape(1)
    fixed = (lam, edge, mine)
    small = (marks, taps, conv_bias, par, skip, gain, pick, down_in, up_in, up_wide, down_out, up_out, fixed)
    tokens_near, cot_q, small = tie(tokens_near, cot_q, small)
    marks, taps, conv_bias, par, skip, gain, pick, down_in, up_in, up_wide, down_out, up_out, fixed = small
    lam, edge, mine = fixed
    tokens_far, cot_s = tie(ring_far(tokens_near, "tensor"), delivered(cot_q, "context"))
    cot_s = jnp.concatenate(cot_s, 0)
    cot_parts = shared(cot_s, "tensor")
    normed, gx, rank_t, part, y, xc, bc, slope, g2, states, out_all = run_forward(
        me, (tokens_s, *tokens_near, *tokens_far), input_norm_gain[None], down_in, up_wide, full, down_out,
        marks, taps, conv_bias, par, skip, gain,
    )
    g2, out_all, cot_parts = tie(g2, out_all, cot_parts)
    out_sum = lax.psum_scatter(out_all.reshape(length, width), "tensor", scatter_dimension=0, tiled=True)
    dn, stats, cot, d_low_t = run_pull_back(me, cot_parts, full, up_out, g2, part, down_out)
    stats_all = shared(stats, "tensor")

    backward = lambda half, *carried, **more: run_backward(
        me, half, gx, xc, bc, slope, y, dn, states, stats_all, marks, taps, par, skip, gain, pick,
        full, down_in, up_in, rank_t, *carried, **more,
    )
    *late, lam, edge, late_up, out_grads = backward(1, lam, edge, cot=cot, g2=g2, low_t=d_low_t)
    lam, late = tie(lam, late)
    late_parts = delivered(late, "tensor")
    *early, _, _, early_up = backward(0, lam, edge)
    early, late_parts, out_sum = tie(early, late_parts, out_sum)
    early_parts = delivered(early, "tensor")
    scratch = pltpu.VMEM((length, SUB), F32)
    branch = run_to_context(finish_branch, me, (out_sum, *stats_all, up_out), share, width, scratch, "finish_branch")
    branch_parts = delivered(branch, "context")
    early_parts, branch_parts = tie(early_parts, branch_parts)
    branch_q = jnp.stack(branch_parts)
    out_near = ring_near(branch_q, "tensor")
    *d_in, sent = run_in_grads(
        jnp.concatenate([me, mine]), early_parts, late_parts, early_up, late_up, normed, out_grads, share
    )
    sent_all = lax.all_gather(sent, ("fsdp", "context"), axis=0, tiled=True)
    d_in_parts = delivered(d_in, "context")
    d_in_parts, out_near, sent = tie(d_in_parts, out_near, sent)
    d_in_q = jnp.stack(d_in_parts)
    d_in_near = ring_near(d_in_q, "tensor")
    out_far = ring_far(out_near, "tensor")
    d_in_near, out_far = tie(d_in_near, out_far)
    d_in_far = ring_far(d_in_near, "tensor")
    layer_out = run_finish(finish_out, me, (branch_q, *out_near, *out_far), (tokens,), BF, "finish_out")
    table = in_adapter_down.shape[0]
    tables = run_tables(sent_all, table, rank, ((width,), (2, inner), (inner,), (width,)))
    layer_out, d_in_far, tables = tie(layer_out, d_in_far, tables)
    grad_tokens = run_finish(
        finish_grad, me, (d_in_q, *d_in_near, *d_in_far), (tokens, output_cotangent, input_norm_gain[None]), F32, "finish_grad"
    )
    return (
        layer_out,
        grad_tokens,
        tables[0].transpose(0, 2, 1),
        tables[1],
        tables[2].transpose(0, 2, 1),
        tables[3],
    )


def solution(mesh):
    placed = (
        P("fsdp", "context", None),
        P("fsdp", "context", None),
        P("fsdp", "context"),
        P("fsdp"),
        P(),
        P(("fsdp", "context"), None, "tensor"),
        P(("fsdp", "context"), None),
        P(("fsdp", "context"), "tensor"),
        P(None, "tensor"),
        P("tensor"),
        P(),
        P(),
        P("tensor"),
        P("tensor"),
        P("tensor"),
        P("tensor"),
        P("tensor", ("fsdp", "context")),
        P(),
        P(None, None, None, "tensor"),
        P(None, "tensor", None),
        P(),
    )
    return jax.shard_map(
        per_device,
        mesh=mesh,
        in_specs=placed,
        out_specs=(
            P("fsdp", "context", None),
            P("fsdp", "context", None),
            P(),
            P(None, None, None, "tensor"),
            P(None, "tensor", None),
            P(),
        ),
        check_vma=False,
    )
```

time: 391 us -> 302 us (0.77)
  Pallas kernels: 32.6 us -> 115 us
  waiting for transfers between devices: 139 us -> 84.1 us
  matrix products: 51.6 us -> 0 us
  other arithmetic: 25.7 us -> 6.79 us
  local copies, waits for them, and re-layouts: 40.4 us -> 21.8 us
  starting transfers between devices: 70 us -> 52.4 us
  blocking collectives: 8.11 us -> 0 us
    pallas_call x2 -> x9, Pallas kernels: 32.6 us -> 115 us  [the longest x2 39.5 us: run_backward(): pl.pallas_call(functools.partial(backward_half, with_grads=with_grads), g...]
    dot_general x17 -> x0, matrix products: 51.6 us -> none  [the longest x7 28 us: dot_nn(): lax.dot_general(a, b, (((1,), (0,)), ((), ())), preferred_element_type=F32)]
    ppermute x24 -> x33, waiting for transfers between devices: 111 us -> 70.9 us  [shifted_by(): lax.ppermute(value, axis, [(i, (i + distance) % size) for i in range(size)])]
    all_to_all x5 -> x2, starting transfers between devices: 22.4 us -> 8.64 us  [swapped(): return lax.all_to_all(value, axis, 0, 0, tiled=True)]
    all_to_all x5 -> x2, waiting for transfers between devices: 26.7 us -> 13.1 us  [swapped(): return lax.all_to_all(value, axis, 0, 0, tiled=True)]
    unnamed x77 -> x90, local copies, waits for them, and re-layouts: 13.4 us -> 4.66 us
    unnamed x1 -> x0, blocking collectives: 8.11 us -> none
    convert_element_type x5 -> x0, other arithmetic: 8.06 us -> none  [the longest x1 2.64 us: per_device(): collect(by_owner(d_in), 'tensor').astype(BF)]
  transfers between devices with their start and end apart: 32 -> 38, of which waited for: 12 -> 15; matrix products, arithmetic and copies ran while one was open for 19% -> 7% of each run, Pallas kernels for 5% -> 34%
where the time goes in v2:
time: 302 us; the launch traced here: 296 us
  Pallas kernels  115 us (38%)
  waiting for transfers between devices  84.1 us (28%)
  starting transfers between devices  52.4 us (17%)
  local copies, waits for them, and re-layouts  21.8 us (7%)
  between operations  16.6 us (5%)
  other arithmetic  6.79 us (2%)
    ppermute x33, waiting for transfers between devices, shifted_by(): lax.ppermute(value, axis, [(i, (i + distance) % size) for i in range(size)])  70.9 us
    ppermute x33, starting transfers between devices, shifted_by(): lax.ppermute(value, axis, [(i, (i + distance) % size) for i in range(size)])  43.6 us
    pallas_call x2, Pallas kernels, run_backward(): pl.pallas_call(functools.partial(backward_half, with_grads=with_grads), g...  39.5 us
    pallas_call x1, Pallas kernels, run_forward(): pl.pallas_call(forward_all, grid_spec=pltpu.PrefetchScalarGridSpec(num_sc...  36.3 us
    pallas_call x2, Pallas kernels, run_finish(): pl.pallas_call(kernel, grid_spec=pltpu.PrefetchScalarGridSpec(num_scalar_...  14.3 us
    all_to_all x2, waiting for transfers between devices, swapped(): return lax.all_to_all(value, axis, 0, 0, tiled=True)  13.1 us
    pallas_call x1, Pallas kernels, run_pull_back(): pl.pallas_call(pull_back, grid_spec=pltpu.PrefetchScalarGridSpec(num_scal...  10.2 us
    all_to_all x2, starting transfers between devices, swapped(): return lax.all_to_all(value, axis, 0, 0, tiled=True)  8.64 us
  transfers between devices with their start and end apart: 38, of which 15 were waited for; matrix products, arithmetic and copies ran while one was open for 7% of the time, Pallas kernels for 34%

profile of v2, /device:TPU:0, one launch (start us, length us, event | category | flops | bytes accessed | tf_op | source)
XLA Modules:
  0.0 296.2 jit_solution(15051313754148162290)
XLA Ops:
  10.9 2.1 constant_dynamic-slice_fusion.5
  12.9 5.4 %all-to-all-start = ((bf16[4,64,1536]{2,1,0:T(8,128)(2,1)}), bf16[4,64,1536]{2,1,0:T(8,128)(2,1)S(1)}, u32[]{:S(2)}, u32[]{:S(2)}) async-start(bf16[4,64,1536]{2,1,0:T(8,128)(2,1)} %constant_dynamic-slice_fusion.5), calls=%async_computation | async-start | bytes 1572864 | tf_op jit(solution)/shard_map/all_to_all | solution.py:852
  19.2 13.1 %all-to-all-done.p0 = bf16[4,64,1536]{2,1,0:T(8,128)(2,1)S(1)} async-done(((bf16[4,64,1536]{2,1,0:T(8,128)(2,1)}), bf16[4,64,1536]{2,1,0:T(8,128)(2,1)S(1)}, u32[]{:S(2)}, u32[]{:S(2)}) %all-to-all-start) | async-done | bytes 786464 | tf_op jit(solution)/shard_map/all_to_all | solution.py:852
  32.3 3.1 %collective-permute-start.1 = (bf16[4,64,1536]{2,1,0:T(8,128)(2,1)S(1)}, bf16[4,64,1536]{2,1,0:T(8,128)(2,1)S(1)}, u32[]{:S(2)}, u32[]{:S(2)}) collective-permute-start(bf16[4,64,1536]{2,1,0:T(8,128)(2,1)S(1)} %all-to-all-done.p0), channel_id=1, source_target_pairs={{0,3},{1,0},{2,1},{3,2},{4,7},{5,4},{6,5},{7,6},{8,11},{9,8},{10,9... | collective-permute-start | bytes 2359304 | tf_op jit(solution)/shard_map/ppermute | solution.py:823
  37.7 3.2 %all-to-all-start.1 = ((s32[4,1,256]{2,1,0:T(1,128)}), s32[4,1,256]{2,1,0:T(1,128)S(1)}, u32[]{:S(2)}, u32[]{:S(2)}) async-start(s32[4,1,256]{2,1,0:T(1,128)} %all_to_all.10), calls=%async_computation.1 | async-start | bytes 8192 | tf_op jit(solution)/shard_map/all_to_all | solution.py:852
  54.1 2.9 collective-permute-start.3
  59.0 2.7 collective-permute-start.5
  63.1 6.7 %collective-permute-done.4 = bf16[1,64,1536]{2,1,0:T(8,128)(2,1)S(1)} collective-permute-done((bf16[1,64,1536]{2,1,0:T(8,128)(2,1)S(1)}, bf16[1,64,1536]{2,1,0:T(8,128)(2,1)S(1)}, u32[]{:S(2)}, u32[]{:S(2)}) %collective-permute-start.4) | collective-permute-done | bytes 196640 | tf_op jit(solution)/shard_map/ppermute | solution.py:823
  69.8 4.4 %collective-permute-done.5 = bf16[1,64,1536]{2,1,0:T(8,128)(2,1)S(1)} collective-permute-done((bf16[1,64,1536]{2,1,0:T(8,128)(2,1)S(1)}, bf16[1,64,1536]{2,1,0:T(8,128)(2,1)S(1)}, u32[]{:S(2)}, u32[]{:S(2)}) %collective-permute-start.5) | collective-permute-done | bytes 196640 | tf_op jit(solution)/shard_map/ppermute | solution.py:823
  75.1 2.8 collective-permute-start.9
  82.1 36.3 %forward_all.1 = (bf16[1024,1536]{1,0:T(8,128)(2,1)}, bf16[1024,2048]{1,0:T(8,128)(2,1)}, bf16[16,1024]{1,0:T(8,128)(2,1)}, f32[24,1024]{1,0:T(8,128)}, bf16[102...) custom-call(s32[2]{0:T(128)} %pad_add_fusion.me_ref, ...), custom_call_target="tpu_custom_call" | custom-call | flops 3000000000 | bytes 9000000 | tf_op jit(solution)/shard_map/forward_all/pallas_call | solution.py:441
  118.5 10.2 %pull_back.1 = (bf16[1024,768]{1,0:T(8,128)(2,1)}, f32[24,1024]{1,0:T(8,128)}, bf16[1024,1536]{1,0:T(8,128)(2,1)}, bf16[16,1024]{1,0:T(8,128)(2,1)}) custom-call(s32[2]{0:T(128)} %pad_add_fusion.me_ref, bf16[4,64,1536]{2,1,0:T(8,128)(2,1)} %copy-done.16, bf16[4,64,1536]{2,1,0:T(8,128)(2,1)} %collective-permute-done.7.p1, ...), custom_call_target="tpu_custom_call" | custom-call | flops 800000000 | bytes 2400000 | tf_op jit(solution)/shard_map/pull_back/pallas_call | solution.py:530
  128.7 2.4 collective-permute-start.12
  132.9 3.9 %collective-permute-done.12.s3_ref.rest_9_.s3 = f32[24,1024]{1,0:T(8,128)S(1)} collective-permute-done((f32[24,1024]{1,0:T(8,128)}, f32[24,1024]{1,0:T(8,128)S(1)}, u32[]{:S(2)}, u32[]{:S(2)}) %collective-permute-start.12) | collective-permute-done | bytes 98336 | tf_op jit(solution)/shard_map/ppermute | solution.py:823
  136.7 3.8 %collective-permute-done.11.s2_ref.rest_8_.s2 = f32[24,1024]{1,0:T(8,128)S(1)} collective-permute-done((f32[24,1024]{1,0:T(8,128)}, f32[24,1024]{1,0:T(8,128)S(1)}, u32[]{:S(2)}, u32[]{:S(2)}) %collective-permute-start.11) | collective-permute-done | bytes 98336 | tf_op jit(solution)/shard_map/ppermute | solution.py:823
  143.3 20.8 %backward_half.2 = (bf16[144,1536]{1,0:T(8,128)(2,1)}, bf16[144,1536]{1,0:T(8,128)(2,1)}, bf16[144,1536]{1,0:T(8,128)(2,1)}, bf16[144,1536]{1,0:T(8,128)(2,1)}, ...) custom-call(s32[2]{0:T(128)} %pad_add_fusion.me_ref, ...), custom_call_target="tpu_custom_call" | custom-call | flops 1900000000 | bytes 5700000 | tf_op jit(solution)/shard_map/backward_half/pallas_call | solution.py:631
  164.1 2.0 collective-permute-start.13
  166.0 2.0 collective-permute-start.14
  168.8 18.7 %backward_half.3 = (bf16[144,1536]{1,0:T(8,128)(2,1)}, bf16[144,1536]{1,0:T(8,128)(2,1)}, bf16[144,1536]{1,0:T(8,128)(2,1)}, bf16[144,1536]{1,0:T(8,128)(2,1)}, ...) custom-call(s32[2]{0:T(128)} %pad_add_fusion.me_ref, ...), custom_call_target="tpu_custom_call" | custom-call | flops 1900000000 | bytes 5700000 | tf_op jit(solution)/shard_map/backward_half/pallas_call | solution.py:631
  191.8 3.5 %finish_branch.1 = (bf16[64,1536]{1,0:T(8,128)(2,1)}, bf16[64,1536]{1,0:T(8,128)(2,1)}, bf16[64,1536]{1,0:T(8,128)(2,1)}, bf16[64,1536]{1,0:T(8,128)(2,1)}) custom-call(s32[2]{0:T(128)} %pad_add_fusion.me_ref, bf16[256,1536]{1,0:T(8,128)(2,1)} %reduce-scatter.2.cloned.1.call-done.sum_ref, f32[24,1024]{1,0:T(8,128)} %get-tuple-element.212.s0_ref.rest_6_.s0, ...), custom_call_target="tpu_custom_call" | custom-call | flops 300000000 | bytes 900000 | tf_op jit(solution)/shard_map/finish_branch/pallas_call | solution.py:687
  195.3 2.0 collective-permute-start.20
  197.2 7.2 %collective-permute-done.19 = bf16[64,1536]{1,0:T(8,128)(2,1)S(1)} collective-permute-done((bf16[64,1536]{1,0:T(8,128)(2,1)}, bf16[64,1536]{1,0:T(8,128)(2,1)S(1)}, u32[]{:S(2)}, u32[]{:S(2)}) %collective-permute-start.19) | collective-permute-done | bytes 196640 | tf_op jit(solution)/shard_map/ppermute | solution.py:823
  205.7 4.7 %collective-permute-done.21 = bf16[64,1536]{1,0:T(8,128)(2,1)S(1)} collective-permute-done((bf16[64,1536]{1,0:T(8,128)(2,1)}, bf16[64,1536]{1,0:T(8,128)(2,1)S(1)}, u32[]{:S(2)}, u32[]{:S(2)}) %collective-permute-start.21) | collective-permute-done | bytes 196640 | tf_op jit(solution)/shard_map/ppermute | solution.py:823
  211.4 5.9 %in_grads.1 = (bf16[64,1536]{1,0:T(8,128)(2,1)}, bf16[64,1536]{1,0:T(8,128)(2,1)}, bf16[64,1536]{1,0:T(8,128)(2,1)}, bf16[64,1536]{1,0:T(8,128)(2,1)}, bf16[16,5504]{1,0:T(8,128)(2,1)}) custom-call(s32[3]{0:T(128)} %pad_add_fusion.2.me_ref, bf16[144,1536]{1,0:T(8,128)(2,1)} %get-tuple-element.250.refs_0_, bf16[144,1536]{1,0:T(8,128)(2,1)} %copy-done.21, ...), custom_call_target="tpu_custom_call" | custom-call | flops 300000000 | bytes 900000 | tf_op jit(solution)/shard_map/in_grads/pallas_call | solution.py:729
  219.9 2.7 collective-permute-start.23
  223.1 7.8 %collective-permute-done.22 = bf16[64,1536]{1,0:T(8,128)(2,1)S(1)} collective-permute-done((bf16[64,1536]{1,0:T(8,128)(2,1)}, bf16[64,1536]{1,0:T(8,128)(2,1)S(1)}, u32[]{:S(2)}, u32[]{:S(2)}) %collective-permute-start.22) | collective-permute-done | bytes 196640 | tf_op jit(solution)/shard_map/ppermute | solution.py:823
  231.9 3.2 %collective-permute-done.26.p2 = bf16[4,64,1536]{2,1,0:T(8,128)(2,1)S(1)} collective-permute-done((bf16[4,64,1536]{2,1,0:T(8,128)(2,1)S(1)}, bf16[4,64,1536]{2,1,0:T(8,128)(2,1)S(1)}, u32[]{:S(2)}, u32[]{:S(2)}) %collective-permute-start.26) | collective-permute-done | bytes 786464 | tf_op jit(solution)/shard_map/ppermute | solution.py:823
  235.1 3.4 %collective-permute-done.25.p1 = bf16[4,64,1536]{2,1,0:T(8,128)(2,1)S(1)} collective-permute-done((bf16[4,64,1536]{2,1,0:T(8,128)(2,1)S(1)}, bf16[4,64,1536]{2,1,0:T(8,128)(2,1)S(1)}, u32[]{:S(2)}, u32[]{:S(2)}) %collective-permute-start.25) | collective-permute-done | bytes 786464 | tf_op jit(solution)/shard_map/ppermute | solution.py:823
  244.0 21.6 %collective-permute-done.30.p4 = bf16[2,64,1536]{2,1,0:T(8,128)(2,1)S(1)} collective-permute-done((bf16[2,64,1536]{2,1,0:T(8,128)(2,1)S(1)}, bf16[2,64,1536]{2,1,0:T(8,128)(2,1)S(1)}, u32[]{:S(2)}, u32[]{:S(2)}) %collective-permute-start.30) | collective-permute-done | bytes 393248 | tf_op jit(solution)/shard_map/ppermute | solution.py:823
  269.3 5.9 %finish_out.1 = bf16[4,256,1536]{2,1,0:T(8,128)(2,1)} custom-call(s32[2]{0:T(128)S(1)} %copy-done.3, bf16[4,64,1536]{2,1,0:T(8,128)(2,1)} %copy-done.5, bf16[4,64,1536]{2,1,0:T(8,128)(2,1)} %copy-done.10, bf16[4,64,1536]{2,1,0:T(8,128)(2,1)} %copy-done.9, bf16[2,64,1536]{2,1,0:T(8,128)(2,1)} %copy-done.26, bf16[2,64,1536]{2,1,0:T(8,128)(2,1)} %copy-done.25, ...), custom_call_target="tpu_custom_call" | custom-call | flops 500000000 | bytes 1500000 | tf_op jit(solution)/shard_map/finish_out/pallas_call | solution.py:775
  275.3 4.7 %fill_tables.1 = (f32[8,16,1536]{2,1,0:T(8,128)}, f32[8,16,2,768]{3,2,1,0:T(2,128)}, f32[8,16,768]{2,1,0:T(8,128)}, f32[8,16,1536]{2,1,0:T(8,128)}) custom-call(bf16[512,5504]{1,0:T(8,128)(2,1)} %all-gather.5.cloned.1.call-done.all_ref), custom_call_target="tpu_custom_call" | custom-call | flops 300000000 | bytes 900000 | tf_op jit(solution)/shard_map/fill_tables/pallas_call | solution.py:812
  280.8 8.4 %finish_grad.1 = f32[4,256,1536]{2,1,0:T(8,128)} custom-call(s32[2]{0:T(128)S(1)} %copy-done.3, bf16[4,64,1536]{2,1,0:T(8,128)(2,1)} %copy-done.4, bf16[4,64,1536]{2,1,0:T(8,128)(2,1)} %copy-done.8, bf16[4,64,1536]{2,1,0:T(8,128)(2,1)} %copy-done.7, bf16[2,64,1536]{2,1,0:T(8,128)(2,1)} %collective-permute-done.31.p3, bf16[2,64,1536]{2,1,0:T(8,128)(2,1)} %copy-done.27, ...), custom_call_target="tpu_custom_call" | custom-call | flops 500000000 | bytes 1500000 | tf_op jit(solution)/shard_map/finish_grad/pallas_call | solution.py:775
  (200 shorter events, 52.1 us)
Async XLA Ops:
  7.2 74.8 %all-gather.3.cloned.1.call-start = ((), (), s32[]{:S(2)}) async-start(), calls=%async_computation.3 | async-start | bytes 8515584 | tf_op jit(solution)/shard_map/all_gather | solution.py:883
  12.9 19.3 %all-to-all-start = ((bf16[4,64,1536]{2,1,0:T(8,128)(2,1)}), bf16[4,64,1536]{2,1,0:T(8,128)(2,1)S(1)}, u32[]{:S(2)}, u32[]{:S(2)}) async-start(bf16[4,64,1536]{2,1,0:T(8,128)(2,1)} %constant_dynamic-slice_fusion.5), calls=%async_computation | async-start | bytes 1572864 | tf_op jit(solution)/shard_map/all_to_all | solution.py:852
  32.3 21.4 %collective-permute-start.1 = (bf16[4,64,1536]{2,1,0:T(8,128)(2,1)S(1)}, bf16[4,64,1536]{2,1,0:T(8,128)(2,1)S(1)}, u32[]{:S(2)}, u32[]{:S(2)}) collective-permute-start(bf16[4,64,1536]{2,1,0:T(8,128)(2,1)S(1)} %all-to-all-done.p0), channel_id=1, source_target_pairs={{0,3},{1,0},{2,1},{3,2},{4,7},{5,4},{6,5},{7,6},{8,11},{9,8},{10,9... | collective-permute-start | bytes 2359304 | tf_op jit(solution)/shard_map/ppermute | solution.py:823
  35.4 18.7 %collective-permute-start = (bf16[4,64,1536]{2,1,0:T(8,128)(2,1)S(1)}, bf16[4,64,1536]{2,1,0:T(8,128)(2,1)S(1)}, u32[]{:S(2)}, u32[]{:S(2)}) collective-permute-start(bf16[4,64,1536]{2,1,0:T(8,128)(2,1)S(1)} %all-to-all-done.p0), channel_id=1, source_target_pairs={{0,1},{1,2},{2,3},{3,0},{4,5},{5,6},{6,7},{7,4},{8,9},{9,10},{10,1... | collective-permute-start | bytes 2359304 | tf_op jit(solution)/shard_map/ppermute | solution.py:823
  37.7 12.8 %all-to-all-start.1 = ((s32[4,1,256]{2,1,0:T(1,128)}), s32[4,1,256]{2,1,0:T(1,128)S(1)}, u32[]{:S(2)}, u32[]{:S(2)}) async-start(s32[4,1,256]{2,1,0:T(1,128)} %all_to_all.10), calls=%async_computation.1 | async-start | bytes 8192 | tf_op jit(solution)/shard_map/all_to_all | solution.py:852
  40.9 146.7 %reduce-scatter.2.cloned.1.call-start = ((), (), s32[]{:S(2)}) async-start(), calls=%async_computation.4 | async-start | bytes 3932160 | tf_op jit(solution)/shard_map/reduce_scatter | solution.py:951
  54.1 20.1 %collective-permute-start.3 = (bf16[2,64,1536]{2,1,0:T(8,128)(2,1)S(1)}, bf16[2,64,1536]{2,1,0:T(8,128)(2,1)S(1)}, u32[]{:S(2)}, u32[]{:S(2)}) collective-permute-start(bf16[2,64,1536]{2,1,0:T(8,128)(2,1)S(1)} %slice.127), channel_id=1, source_target_pairs={{0,3},{1,0},{2,1},{3,2},{4,7},{5,4},{6,5},{7,6},{8,11},{9,8},{10,9... | collective-permute-start | bytes 1179656 | tf_op jit(solution)/shard_map/ppermute | solution.py:823
  57.0 18.0 %collective-permute-start.2 = (bf16[2,64,1536]{2,1,0:T(8,128)(2,1)S(1)}, bf16[2,64,1536]{2,1,0:T(8,128)(2,1)}, u32[]{:S(2)}, u32[]{:S(2)}) collective-permute-start(bf16[2,64,1536]{2,1,0:T(8,128)(2,1)S(1)} %slice.126), channel_id=1, source_target_pairs={{0,1},{1,2},{2,3},{3,0},{4,5},{5,6},{6,7},{7,4},{8,9},{9,10},{10,1... | collective-permute-start | bytes 1179656 | tf_op jit(solution)/shard_map/ppermute | solution.py:823
  57.0 12.8 %collective-permute-start.4 = (bf16[1,64,1536]{2,1,0:T(8,128)(2,1)S(1)}, bf16[1,64,1536]{2,1,0:T(8,128)(2,1)S(1)}, u32[]{:S(2)}, u32[]{:S(2)}) collective-permute-start(bf16[1,64,1536]{2,1,0:T(8,128)(2,1)S(1)} %get-tuple-element.178), channel_id=1, source_target_pairs={{0,4},{4,8},{8,12},{12,0},{1,5},{5,9},{9,13},{13,1},{2,6},{6,10},{... | collective-permute-start | bytes 589832 | tf_op jit(solution)/shard_map/ppermute | solution.py:823
  59.0 15.3 %collective-permute-start.5 = (bf16[1,64,1536]{2,1,0:T(8,128)(2,1)S(1)}, bf16[1,64,1536]{2,1,0:T(8,128)(2,1)S(1)}, u32[]{:S(2)}, u32[]{:S(2)}) collective-permute-start(bf16[1,64,1536]{2,1,0:T(8,128)(2,1)S(1)} %get-tuple-element.179), channel_id=1, source_target_pairs={{0,8},{4,12},{8,0},{12,4},{1,9},{5,13},{9,1},{13,5},{2,10},{6,14},... | collective-permute-start | bytes 589832 | tf_op jit(solution)/shard_map/ppermute | solution.py:823
  61.7 12.6 %collective-permute-start.6 = (bf16[1,64,1536]{2,1,0:T(8,128)(2,1)S(1)}, bf16[1,64,1536]{2,1,0:T(8,128)(2,1)S(1)}, u32[]{:S(2)}, u32[]{:S(2)}) collective-permute-start(bf16[1,64,1536]{2,1,0:T(8,128)(2,1)S(1)} %get-tuple-element.180), channel_id=1, source_target_pairs={{0,12},{4,0},{8,4},{12,8},{1,13},{5,1},{9,5},{13,9},{2,14},{6,2},{... | collective-permute-start | bytes 589832 | tf_op jit(solution)/shard_map/ppermute | solution.py:823
  75.1 43.3 %collective-permute-start.9 = (bf16[4,64,1536]{2,1,0:T(8,128)(2,1)S(1)}, bf16[4,64,1536]{2,1,0:T(8,128)(2,1)}, u32[]{:S(2)}, u32[]{:S(2)}) collective-permute-start(bf16[4,64,1536]{2,1,0:T(8,128)(2,1)S(1)} %constant_dynamic-update-slice_fusion.p0), channel_id=1, source_target_pairs={{0,3},{1,0},{2,1},{3,2},{4,7},{5,4},{6,5},{7,6},{8,11},{9,8},{10,9... | collective-permute-start | bytes 2359304 | tf_op jit(solution)/shard_map/ppermute | solution.py:823
  77.9 40.5 %collective-permute-start.8 = (bf16[4,64,1536]{2,1,0:T(8,128)(2,1)S(1)}, bf16[4,64,1536]{2,1,0:T(8,128)(2,1)}, u32[]{:S(2)}, u32[]{:S(2)}) collective-permute-start(bf16[4,64,1536]{2,1,0:T(8,128)(2,1)S(1)} %constant_dynamic-update-slice_fusion.p0), channel_id=1, source_target_pairs={{0,2},{1,3},{2,0},{3,1},{4,6},{5,7},{6,4},{7,5},{8,10},{9,11},{10,... | collective-permute-start | bytes 2359304 | tf_op jit(solution)/shard_map/ppermute | solution.py:823
  78.7 39.7 %collective-permute-start.7 = (bf16[4,64,1536]{2,1,0:T(8,128)(2,1)S(1)}, bf16[4,64,1536]{2,1,0:T(8,128)(2,1)}, u32[]{:S(2)}, u32[]{:S(2)}) collective-permute-start(bf16[4,64,1536]{2,1,0:T(8,128)(2,1)S(1)} %constant_dynamic-update-slice_fusion.p0), channel_id=1, source_target_pairs={{0,1},{1,2},{2,3},{3,0},{4,5},{5,6},{6,7},{7,4},{8,9},{9,10},{10,1... | collective-permute-start | bytes 2359304 | tf_op jit(solution)/shard_map/ppermute | solution.py:823
  118.5 156.9 %all-gather.5.cloned.1.call-start = ((), (), s32[]{:S(2)}) async-start(), calls=%async_computation.5 | async-start | bytes 5812224 | tf_op jit(solution)/shard_map/all_gather | solution.py:974
  164.1 23.5 %collective-permute-start.13 = (bf16[144,1536]{1,0:T(8,128)(2,1)}, bf16[144,1536]{1,0:T(8,128)(2,1)S(1)}, u32[]{:S(2)}, u32[]{:S(2)}) collective-permute-start(bf16[144,1536]{1,0:T(8,128)(2,1)} %get-tuple-element.232), channel_id=1, source_target_pairs={{0,1},{1,2},{2,3},{3,0},{4,5},{5,6},{6,7},{7,4},{8,9},{9,10},{10,1... | collective-permute-start | bytes 1327112 | tf_op jit(solution)/shard_map/ppermute | solution.py:823
  166.0 21.5 %collective-permute-start.14 = (bf16[144,1536]{1,0:T(8,128)(2,1)}, bf16[144,1536]{1,0:T(8,128)(2,1)S(1)}, u32[]{:S(2)}, u32[]{:S(2)}) collective-permute-start(bf16[144,1536]{1,0:T(8,128)(2,1)} %get-tuple-element.233), channel_id=1, source_target_pairs={{0,2},{1,3},{2,0},{3,1},{4,6},{5,7},{6,4},{7,5},{8,10},{9,11},{10,... | collective-permute-start | bytes 1327112 | tf_op jit(solution)/shard_map/ppermute | solution.py:823
  168.0 19.6 %collective-permute-start.15 = (bf16[144,1536]{1,0:T(8,128)(2,1)}, bf16[144,1536]{1,0:T(8,128)(2,1)S(1)}, u32[]{:S(2)}, u32[]{:S(2)}) collective-permute-start(bf16[144,1536]{1,0:T(8,128)(2,1)} %get-tuple-element.234), channel_id=1, source_target_pairs={{0,3},{1,0},{2,1},{3,2},{4,7},{5,4},{6,5},{7,6},{8,11},{9,8},{10,9... | collective-permute-start | bytes 1327112 | tf_op jit(solution)/shard_map/ppermute | solution.py:823
  187.6 22.7 %collective-permute-start.16 = (bf16[144,1536]{1,0:T(8,128)(2,1)}, bf16[144,1536]{1,0:T(8,128)(2,1)S(1)}, u32[]{:S(2)}, u32[]{:S(2)}) collective-permute-start(bf16[144,1536]{1,0:T(8,128)(2,1)} %get-tuple-element.237), channel_id=1, source_target_pairs={{0,1},{1,2},{2,3},{3,0},{4,5},{5,6},{6,7},{7,4},{8,9},{9,10},{10,1... | collective-permute-start | bytes 1327112 | tf_op jit(solution)/shard_map/ppermute | solution.py:823
  188.9 21.5 %collective-permute-start.17 = (bf16[144,1536]{1,0:T(8,128)(2,1)}, bf16[144,1536]{1,0:T(8,128)(2,1)S(1)}, u32[]{:S(2)}, u32[]{:S(2)}) collective-permute-start(bf16[144,1536]{1,0:T(8,128)(2,1)} %get-tuple-element.238), channel_id=1, source_target_pairs={{0,2},{1,3},{2,0},{3,1},{4,6},{5,7},{6,4},{7,5},{8,10},{9,11},{10,... | collective-permute-start | bytes 1327112 | tf_op jit(solution)/shard_map/ppermute | solution.py:823
  190.5 19.9 %collective-permute-start.18 = (bf16[144,1536]{1,0:T(8,128)(2,1)}, bf16[144,1536]{1,0:T(8,128)(2,1)S(1)}, u32[]{:S(2)}, u32[]{:S(2)}) collective-permute-start(bf16[144,1536]{1,0:T(8,128)(2,1)} %get-tuple-element.239), channel_id=1, source_target_pairs={{0,3},{1,0},{2,1},{3,2},{4,7},{5,4},{6,5},{7,6},{8,11},{9,8},{10,9... | collective-permute-start | bytes 1327112 | tf_op jit(solution)/shard_map/ppermute | solution.py:823
  195.3 10.4 %collective-permute-start.20 = (bf16[64,1536]{1,0:T(8,128)(2,1)}, bf16[64,1536]{1,0:T(8,128)(2,1)S(1)}, u32[]{:S(2)}, u32[]{:S(2)}) collective-permute-start(bf16[64,1536]{1,0:T(8,128)(2,1)} %get-tuple-element.243), channel_id=1, source_target_pairs={{0,8},{4,12},{8,0},{12,4},{1,9},{5,13},{9,1},{13,5},{2,10},{6,14},... | collective-permute-start | bytes 589832 | tf_op jit(solution)/shard_map/ppermute | solution.py:823
  217.5 17.6 %collective-permute-start.26 = (bf16[4,64,1536]{2,1,0:T(8,128)(2,1)S(1)}, bf16[4,64,1536]{2,1,0:T(8,128)(2,1)S(1)}, u32[]{:S(2)}, u32[]{:S(2)}) collective-permute-start(bf16[4,64,1536]{2,1,0:T(8,128)(2,1)S(1)} %pad_maximum_fusion.p0), channel_id=1, source_target_pairs={{0,3},{1,0},{2,1},{3,2},{4,7},{5,4},{6,5},{7,6},{8,11},{9,8},{10,9... | collective-permute-start | bytes 2359304 | tf_op jit(solution)/shard_map/ppermute | solution.py:823
  219.0 19.5 %collective-permute-start.25 = (bf16[4,64,1536]{2,1,0:T(8,128)(2,1)S(1)}, bf16[4,64,1536]{2,1,0:T(8,128)(2,1)S(1)}, u32[]{:S(2)}, u32[]{:S(2)}) collective-permute-start(bf16[4,64,1536]{2,1,0:T(8,128)(2,1)S(1)} %pad_maximum_fusion.p0), channel_id=1, source_target_pairs={{0,1},{1,2},{2,3},{3,0},{4,5},{5,6},{6,7},{7,4},{8,9},{9,10},{10,1... | collective-permute-start | bytes 2359304 | tf_op jit(solution)/shard_map/ppermute | solution.py:823
  219.9 11.0 %collective-permute-start.22 = (bf16[64,1536]{1,0:T(8,128)(2,1)}, bf16[64,1536]{1,0:T(8,128)(2,1)S(1)}, u32[]{:S(2)}, u32[]{:S(2)}) collective-permute-start(bf16[64,1536]{1,0:T(8,128)(2,1)} %get-tuple-element.263), channel_id=1, source_target_pairs={{0,4},{4,8},{8,12},{12,0},{1,5},{5,9},{9,13},{13,1},{2,6},{6,10},{... | collective-permute-start | bytes 589832 | tf_op jit(solution)/shard_map/ppermute | solution.py:823
  219.9 11.0 %collective-permute-start.23 = (bf16[64,1536]{1,0:T(8,128)(2,1)}, bf16[64,1536]{1,0:T(8,128)(2,1)S(1)}, u32[]{:S(2)}, u32[]{:S(2)}) collective-permute-start(bf16[64,1536]{1,0:T(8,128)(2,1)} %get-tuple-element.264), channel_id=1, source_target_pairs={{0,8},{4,12},{8,0},{12,4},{1,9},{5,13},{9,1},{13,5},{2,10},{6,14},... | collective-permute-start | bytes 589832 | tf_op jit(solution)/shard_map/ppermute | solution.py:823
  239.7 27.4 %collective-permute-start.28 = (bf16[4,64,1536]{2,1,0:T(8,128)(2,1)S(1)}, bf16[4,64,1536]{2,1,0:T(8,128)(2,1)S(1)}, u32[]{:S(2)}, u32[]{:S(2)}) collective-permute-start(bf16[4,64,1536]{2,1,0:T(8,128)(2,1)S(1)} %pad_maximum_fusion.1.p0), channel_id=1, source_target_pairs={{0,3},{1,0},{2,1},{3,2},{4,7},{5,4},{6,5},{7,6},{8,11},{9,8},{10,9... | collective-permute-start | bytes 2359304 | tf_op jit(solution)/shard_map/ppermute | solution.py:823
  240.1 27.0 %collective-permute-start.27 = (bf16[4,64,1536]{2,1,0:T(8,128)(2,1)S(1)}, bf16[4,64,1536]{2,1,0:T(8,128)(2,1)S(1)}, u32[]{:S(2)}, u32[]{:S(2)}) collective-permute-start(bf16[4,64,1536]{2,1,0:T(8,128)(2,1)S(1)} %pad_maximum_fusion.1.p0), channel_id=1, source_target_pairs={{0,1},{1,2},{2,3},{3,0},{4,5},{5,6},{6,7},{7,4},{8,9},{9,10},{10,1... | collective-permute-start | bytes 2359304 | tf_op jit(solution)/shard_map/ppermute | solution.py:823
  241.9 23.7 %collective-permute-start.30 = (bf16[2,64,1536]{2,1,0:T(8,128)(2,1)S(1)}, bf16[2,64,1536]{2,1,0:T(8,128)(2,1)S(1)}, u32[]{:S(2)}, u32[]{:S(2)}) collective-permute-start(bf16[2,64,1536]{2,1,0:T(8,128)(2,1)S(1)} %slice.129), channel_id=1, source_target_pairs={{0,3},{1,0},{2,1},{3,2},{4,7},{5,4},{6,5},{7,6},{8,11},{9,8},{10,9... | collective-permute-start | bytes 1179656 | tf_op jit(solution)/shard_map/ppermute | solution.py:823
  243.5 23.6 %collective-permute-start.29 = (bf16[2,64,1536]{2,1,0:T(8,128)(2,1)S(1)}, bf16[2,64,1536]{2,1,0:T(8,128)(2,1)S(1)}, u32[]{:S(2)}, u32[]{:S(2)}) collective-permute-start(bf16[2,64,1536]{2,1,0:T(8,128)(2,1)S(1)} %slice.128), channel_id=1, source_target_pairs={{0,1},{1,2},{2,3},{3,0},{4,5},{5,6},{6,7},{7,4},{8,9},{9,10},{10,1... | collective-permute-start | bytes 1179656 | tf_op jit(solution)/shard_map/ppermute | solution.py:823
  267.2 12.8 %collective-permute-start.32 = (bf16[2,64,1536]{2,1,0:T(8,128)(2,1)S(1)}, bf16[2,64,1536]{2,1,0:T(8,128)(2,1)S(1)}, u32[]{:S(2)}, u32[]{:S(2)}) collective-permute-start(bf16[2,64,1536]{2,1,0:T(8,128)(2,1)S(1)} %slice.131), channel_id=1, source_target_pairs={{0,3},{1,0},{2,1},{3,2},{4,7},{5,4},{6,5},{7,6},{8,11},{9,8},{10,9... | collective-permute-start | bytes 1179656 | tf_op jit(solution)/shard_map/ppermute | solution.py:823
  267.6 12.5 %collective-permute-start.31 = (bf16[2,64,1536]{2,1,0:T(8,128)(2,1)S(1)}, bf16[2,64,1536]{2,1,0:T(8,128)(2,1)}, u32[]{:S(2)}, u32[]{:S(2)}) collective-permute-start(bf16[2,64,1536]{2,1,0:T(8,128)(2,1)S(1)} %slice.130), channel_id=1, source_target_pairs={{0,1},{1,2},{2,3},{3,0},{4,5},{5,6},{6,7},{7,4},{8,9},{9,10},{10,1... | collective-permute-start | bytes 1179656 | tf_op jit(solution)/shard_map/ppermute | solution.py:823
  (47 other events, 1089.1 us)
Sparse Core Ops, SparseCore 0:
  11.0 61.8 all-gather.2
  118.6 41.2 reduce-scatter.1
  217.5 46.4 all-gather.4
